TPU v7x, 32 devices: a whole 2x2x4 slice. The times are simulated.
32 devices in a mesh: az: 16 (over z, x, core), el: 2 (over y).
Axes of the slice: x: 2, y: 2, z: 4, core: 2. Of those that a mesh axis runs over, the one named last changes fastest.
Arguments:
- raw_sweeps: bfloat16 [4, 1, 24, 96, 256], P('el', None, None, 'az'), may hold values from -6 to 6
- sweep_ids: int32 [4], P('el'), may hold values from 0 to 3, each once
- elevation_embed: float32 [4, 128], replicated, may hold values from -3 to 3
- input_proj: bfloat16 [24, 128], replicated, may hold values from -0.875 to 0.875
- first_kernel: bfloat16 [3, 3, 128, 128], replicated, may hold values from -0.1875 to 0.1875
- second_kernel: bfloat16 [3, 3, 128, 128], replicated, may hold values from -0.1875 to 0.1875
- join_weight: bfloat16 [2, 128, 128], P('el'), may hold values from -0.375 to 0.375
- head_weight: bfloat16 [12, 128], replicated, may hold values from -0.5 to 0.5
- cotangent: bfloat16 [1, 12, 96, 256], P(None, None, 'az'), may hold values from -6 to 6
Outputs:
- prediction: float32 [1, 12, 96, 256], P(None, None, 'az')
- join_grad: float32 [2, 128, 128], P('el')
- first_kernel_gradient: float32 [3, 3, 128, 128], replicated
- second_kernel_gradient: float32 [3, 3, 128, 128], replicated
- input_grad: float32 [24, 128], replicated
- embed_grad: float32 [4, 128], replicated
Inputs may be any that keep to these rules, and one draw needn't show every extreme that they name: `sweep_ids`: each sweep fills exactly one slot.
All inputs are finite; a program needn't handle non-finite values.
Results may differ from a plain program's by a relative error of at most 0.023.
Values may be sent and summed in bfloat16 or wider, within the bound.
A program may use at most 64 MiB of HBM per device.

v0:
```python
import math

import jax
import jax.numpy as jnp
from jax import lax
from jax.sharding import PartitionSpec as P

CHANNELS = 128
FIRST_DILATION = 1
SECOND_DILATION = 2


precise = lax.Precision.HIGHEST


def padded_2(block, sides, width):
    for axis, dim in sides:
        count = lax.axis_size(axis)
        forward = [(i, i + 1) for i in range(count - 1)]
        forward.append((count - 1, 0))
        backward = [(target, source) for source, target in forward]
        low = lax.ppermute(
            lax.slice_in_dim(block, block.shape[dim] - width, None, axis=dim), axis, forward
        )
        high = lax.ppermute(lax.slice_in_dim(block, 0, width, axis=dim), axis, backward)
        block = jnp.concatenate([low, block, high], axis=dim)
    return block


def silu_slope(values):
    logistic = jax.nn.sigmoid(values)
    return logistic * (1.0 + values * (1.0 - logistic))


def range_padding(source, dilate):
    return jnp.pad(source, ((0, 0), (0, 0), (0, 0), (dilate, dilate)))


def convolve_partial(padded, kernel, dilate):
    return lax.conv_general_dilated(
        padded,
        kernel,
        (1, 1),
        "VALID",
        rhs_dilation=(dilate, dilate),
        dimension_numbers=("NCHW", "HWIO", "NCHW"),
        preferred_element_type=jnp.float32,
    )


def reversed_kernel(kernel):
    return jnp.flip(kernel, (0, 1)).transpose(0, 1, 3, 2)


def kernel_gradient_of(padded, upstream, dilate):
    ray_count = upstream.shape[2]
    gate_count = upstream.shape[3]
    tap_rows = []
    for tap_row in range(3):
        tap_line = []
        for tap_column in range(3):
            window = padded[
                :,
                :,
                tap_row * dilate : tap_row * dilate + ray_count,
                tap_column * dilate : tap_column * dilate + gate_count,
            ]
            tap_line.append(
                jnp.einsum("niar,noar->io", window, upstream, preferred_element_type=jnp.float32)
            )
        tap_rows.append(jnp.stack(tap_line))
    return jnp.stack(tap_rows)


def activate(source):
    return jax.nn.silu(source.astype(jnp.float32)).astype(jnp.bfloat16)


def shards(
    raw_sweeps,
    sweep_ids,
    elevation_embed,
    input_proj,
    first_kernel,
    second_kernel,
    join_weight,
    head_weight,
    cotangent,
):
    brain_float_half = jnp.bfloat16
    sweep_total = elevation_embed.shape[0]
    onehot = (sweep_ids[:, None] == jnp.arange(sweep_total, dtype=jnp.int32)[None, :]).astype(
        jnp.float32
    )
    bias_rows = jnp.dot(onehot, elevation_embed, precision=precise)
    group_bias = jnp.sum(bias_rows, axis=0)
    input_state = jnp.einsum(
        "jbiar,ic->bcar", raw_sweeps, input_proj, preferred_element_type=jnp.float32
    )
    input_state = (input_state + group_bias[None, :, None, None]).astype(brain_float_half)
    input_activation = activate(input_state)
    padded_input = range_padding(
        padded_2(input_activation, (("az", 2),), FIRST_DILATION), FIRST_DILATION
    )
    hidden_state = (
        input_state.astype(jnp.float32)
        + convolve_partial(padded_input, first_kernel, FIRST_DILATION)
    ).astype(brain_float_half)
    hidden_activation = activate(hidden_state)
    padded_hidden = range_padding(
        padded_2(hidden_activation, (("az", 2),), SECOND_DILATION), SECOND_DILATION
    )
    final_state = (
        hidden_state.astype(jnp.float32)
        + convolve_partial(padded_hidden, second_kernel, SECOND_DILATION)
    ).astype(brain_float_half)
    group_weight = join_weight[0]
    empty_sum = jnp.zeros((CHANNELS,) + final_state.shape[:1] + final_state.shape[2:], jnp.float32)
    joined_all = (
        empty_sum
        + jnp.einsum(
            "gbiar,gio->obar",
            lax.all_gather(final_state[None], "el", axis=0, tiled=True),
            lax.all_gather(join_weight, "el", axis=0, tiled=True),
            preferred_element_type=jnp.float32,
        )
    ).astype(brain_float_half)
    prediction = jnp.einsum(
        "lc,cbar->blar", head_weight, joined_all, preferred_element_type=jnp.float32
    )
    ray_total = final_state.shape[2] * lax.axis_size("az")
    grad_scale = 1.0 / math.sqrt(
        lax.axis_size("el") * final_state.shape[0] * ray_total * final_state.shape[3]
    )
    joined_back = jnp.einsum(
        "lc,blar->bcar", head_weight, cotangent, preferred_element_type=jnp.float32
    ).astype(brain_float_half)
    join_local = jnp.einsum(
        "biar,boar->io", final_state, joined_back, preferred_element_type=jnp.float32
    )
    join_total = lax.psum(join_local, "az")
    grad_two = jnp.einsum(
        "io,boar->biar", group_weight, joined_back, preferred_element_type=jnp.float32
    )
    final_upstream_gradient = grad_two.astype(brain_float_half)
    second_kernel_partial = kernel_gradient_of(
        padded_hidden, final_upstream_gradient, SECOND_DILATION
    )
    second_border_rays = range_padding(
        padded_2(final_upstream_gradient, (("az", 2),), SECOND_DILATION), SECOND_DILATION
    )
    second_backward_pass = convolve_partial(
        second_border_rays, reversed_kernel(second_kernel), SECOND_DILATION
    )
    grad_one = grad_two + second_backward_pass * silu_slope(hidden_state.astype(jnp.float32))
    hidden_upstream_gradient = grad_one.astype(brain_float_half)
    first_kernel_partial = kernel_gradient_of(
        padded_input, hidden_upstream_gradient, FIRST_DILATION
    )
    first_border_rays = range_padding(
        padded_2(hidden_upstream_gradient, (("az", 2),), FIRST_DILATION), FIRST_DILATION
    )
    first_backward_pass = convolve_partial(
        first_border_rays, reversed_kernel(first_kernel), FIRST_DILATION
    )
    grad_zero = (
        grad_one + first_backward_pass * silu_slope(input_state.astype(jnp.float32))
    ).astype(brain_float_half)
    input_local = jnp.einsum(
        "jbiar,bcar->ic", raw_sweeps, grad_zero, preferred_element_type=jnp.float32
    )
    column_sum = jnp.sum(grad_zero.astype(jnp.float32), axis=(0, 2, 3))
    slot_terms = jnp.broadcast_to(column_sum[None, :], (raw_sweeps.shape[0], column_sum.shape[0]))
    embed_local = jnp.dot(onehot.T, slot_terms, precision=precise)
    second_total, first_total, input_total, embed_total = lax.psum(
        (second_kernel_partial, first_kernel_partial, input_local, embed_local), ("az", "el")
    )
    return (
        prediction,
        join_total[None] * grad_scale,
        first_total * grad_scale,
        second_total * grad_scale,
        input_total * grad_scale,
        embed_total * grad_scale,
    )


def solution(mesh):
    in_specs = (
        P("el", None, None, "az", None),
        P("el"),
        P(),
        P(),
        P(),
        P(),
        P("el", None, None),
        P(),
        P(None, None, "az", None),
    )
    out_specs = (P(None, None, "az", None), P("el", None, None), P(), P(), P(), P())
    return jax.shard_map(shards, mesh=mesh, in_specs=in_specs, out_specs=out_specs, check_vma=False)
```

profile of v0, /device:TPU:1, one launch (start us, length us, event | category | flops | bytes accessed | tf_op | source)
XLA Modules:
  0.0 340.6 jit_solution(14312674388534561637)
XLA Ops:
  7.2 1.0 convert_reduce_fusion.1
  9.1 1.9 fusion.30
  11.1 2.7 collective-permute-start
  14.1 1.2 fusion.177
  15.2 1.8 collective-permute-start.4
  17.0 1.2 collective-permute-start.5
  18.3 3.7 %all_gather.7 = bf16[2,128,128]{2,1,0:T(8,128)(2,1)} all-gather(bf16[1,128,128]{2,1,0:T(8,128)(2,1)S(1)} %copy-done.10), channel_id=1, replica_groups=mesh['az'=16,'el'=2] {'el'}, dimensions={0}, use_global_device_ids=true | all-gather | bytes 98304 | tf_op jit(solution)/shard_map/all_gather | solution.py:124
  23.3 1.1 convolution_select_fusion.3
  24.6 1.0 reshape.182
  27.0 1.1 convolution_select_fusion.1
  29.3 3.1 fusion.170
  36.2 1.7 collective-permute-start.6
  37.9 3.7 %collective-permute-start.7 = (bf16[1,128,1,256]{1,3,2,0:T(8,128)(2,1)S(1)}, bf16[1,128,1,256]{1,3,2,0:T(8,128)(2,1)S(1)}, u32[]{:S(2)}, u32[]{:S(2)}) collective-permute-start(bf16[1,128,1,256]{1,3,2,0:T(8,128)(2,1)S(1)} %get-tuple-element.38), channel_id=1, source_target_pairs={{2,0},{4,2},{6,4},{8,6},{10,8},{12,10},{14,12},{16,14},{18,16},{20... | collective-permute-start | bytes 196616 | tf_op jit(solution)/shard_map/ppermute | solution.py:25
  41.7 4.4 %collective-permute-start.3 = (bf16[1,128,2,256]{1,3,2,0:T(8,128)(2,1)S(1)}, bf16[1,128,2,256]{1,3,2,0:T(8,128)(2,1)S(1)}, u32[]{:S(2)}, u32[]{:S(2)}) collective-permute-start(bf16[1,128,2,256]{1,3,2,0:T(8,128)(2,1)S(1)} %get-tuple-element.40), channel_id=1, source_target_pairs={{2,0},{4,2},{6,4},{8,6},{10,8},{12,10},{14,12},{16,14},{18,16},{20... | collective-permute-start | bytes 393224 | tf_op jit(solution)/shard_map/ppermute | solution.py:25
  48.2 1.1 convolution_select_fusion
  50.4 2.0 convert_reduce_fusion
  52.9 40.2 %all-reduce.2 = (f32[24,128]{1,0:T(8,128)S(1)}, f32[4,128]{1,0:T(4,128)S(1)}) all-reduce(f32[24,128]{1,0:T(8,128)S(1)} %convolution_bitcast_fusion.21, f32[4,128]{1,0:T(4,128)S(1)} %fusion.135), channel_id=1, replica_groups=mesh['az'=16,'el'=2] {'az','el'}, use_global_device_ids=true, to_apply=%region_5.6 | all-reduce | flops 3584 | bytes 28672 | tf_op jit(solution)/shard_map/psum | solution.py:175
  100.1 1.1 convolution_select_fusion.2
  102.4 1.2 fusion.15
  107.2 11.6 %all-gather = bf16[2,128,6,256]{3,1,2,0:T(8,128)(2,1)S(1)} all-gather(bf16[1,128,6,256]{3,1,2,0:T(8,128)(2,1)S(1)} %copy.130), channel_id=2, replica_groups=mesh['az'=16,'el'=2] {'el'}, dimensions={0}, use_global_device_ids=true | all-gather | bytes 1179648 | tf_op jit(solution)/shard_map/all_gather | solution.py:123
  120.2 72.1 %all-reduce.7.cloned.1.call-done = f32[128,128]{1,0:T(8,128)} async-done(((f32[128,128]{1,0:T(8,128)}), f32[128,128]{1,0:T(8,128)}) %all-reduce.7.cloned.1.call-update) | async-done | bytes 65552 | tf_op jit(solution)/shard_map/psum | solution.py:141
  192.3 1.5 multiply_bitcast_fusion
  193.8 137.1 %all-reduce.9.cloned.1.call-done = (f32[3,3,128,128]{3,2,1,0:T(8,128)}, f32[3,3,128,128]{3,2,1,0:T(8,128)}) async-done(((f32[3,3,128,128]{3,2,1,0:T(8,128)}, f32[3,3,128,128]{3,2,1,0:T(8,128)}), (f32[3,3,128,128]{3,2,1,0:T(8,128)}, f32[3,3,128,128]{3,2,1,0:T(8,128)})) %all-reduce.9.cloned.1.call-update) | async-done | bytes 1179664 | tf_op jit(solution)/shard_map/psum | solution.py:175
  330.9 2.0 broadcast_multiply_fusion
  (127 shorter events, 26.5 us)
Async XLA Ops:
  7.2 15.6 %copy-start = (bf16[3,3,128,128]{3,2,1,0:T(8,128)(2,1)S(1)}, bf16[3,3,128,128]{3,2,1,0:T(8,128)(2,1)}, u32[]{:S(2)}) copy-start(bf16[3,3,128,128]{3,2,1,0:T(8,128)(2,1)} %param.13) | copy-start | bytes 884740
  7.2 185.1 %all-reduce.7.cloned.1.call-start = ((), (), s32[]{:S(2)}) async-start(), calls=%async_computation | async-start | bytes 131072 | tf_op jit(solution)/shard_map/psum | solution.py:141
  9.1 4.6 %copy-start.17 = (bf16[1,12,6,256]{3,2,1,0:T(8,128)(2,1)S(1)}, bf16[1,12,6,256]{3,2,1,0:T(8,128)(2,1)}, u32[]{:S(2)}) copy-start(bf16[1,12,6,256]{3,2,1,0:T(8,128)(2,1)} %param.17) | copy-start | bytes 110596
  9.1 4.6 %copy-start.18 = (bf16[12,128]{1,0:T(8,128)(2,1)S(1)}, bf16[12,128]{1,0:T(8,128)(2,1)}, u32[]{:S(2)}) copy-start(bf16[12,128]{1,0:T(8,128)(2,1)} %param.16) | copy-start | bytes 9220
  9.1 4.9 %copy-start.10 = (bf16[1,128,128]{2,1,0:T(8,128)(2,1)S(1)}, bf16[1,128,128]{2,1,0:T(8,128)(2,1)}, u32[]{:S(2)}) copy-start(bf16[1,128,128]{2,1,0:T(8,128)(2,1)} %param.15) | copy-start | bytes 98308
  11.1 10.9 %copy-start.1 = (bf16[128,6,256]{0,2,1:T(8,128)(2,1)}, bf16[128,6,256]{0,2,1:T(8,128)(2,1)S(1)}, u32[]{:S(2)}) copy-start(bf16[128,6,256]{0,2,1:T(8,128)(2,1)S(1)} %get-tuple-element.47) | copy-start | bytes 1179652
  11.1 10.9 %collective-permute-start = (bf16[1,128,1,256]{1,3,2,0:T(8,128)(2,1)S(1)}, bf16[1,128,1,256]{1,3,2,0:T(8,128)(2,1)S(1)}, u32[]{:S(2)}, u32[]{:S(2)}) collective-permute-start(bf16[1,128,1,256]{1,3,2,0:T(8,128)(2,1)S(1)} %get-tuple-element.41), channel_id=1, source_target_pairs={{0,2},{2,4},{4,6},{6,8},{8,10},{10,12},{12,14},{14,16},{16,18},{18... | collective-permute-start | bytes 196616 | tf_op jit(solution)/shard_map/ppermute | solution.py:22
  13.7 8.3 %collective-permute-start.1 = (bf16[1,128,1,256]{1,3,2,0:T(8,128)(2,1)S(1)}, bf16[1,128,1,256]{1,3,2,0:T(8,128)(2,1)S(1)}, u32[]{:S(2)}, u32[]{:S(2)}) collective-permute-start(bf16[1,128,1,256]{1,3,2,0:T(8,128)(2,1)S(1)} %get-tuple-element.42), channel_id=1, source_target_pairs={{2,0},{4,2},{6,4},{8,6},{10,8},{12,10},{14,12},{16,14},{18,16},{20... | collective-permute-start | bytes 196616 | tf_op jit(solution)/shard_map/ppermute | solution.py:25
  15.2 10.4 %collective-permute-start.4 = (bf16[1,128,2,256]{1,3,2,0:T(8,128)(2,1)S(1)}, bf16[1,128,2,256]{1,3,2,0:T(8,128)(2,1)S(1)}, u32[]{:S(2)}, u32[]{:S(2)}) collective-permute-start(bf16[1,128,2,256]{1,3,2,0:T(8,128)(2,1)S(1)} %get-tuple-element.43), channel_id=1, source_target_pairs={{0,2},{2,4},{4,6},{6,8},{8,10},{10,12},{12,14},{14,16},{16,18},{18... | collective-permute-start | bytes 393224 | tf_op jit(solution)/shard_map/ppermute | solution.py:22
  17.0 8.6 %collective-permute-start.5 = (bf16[1,128,2,256]{1,3,2,0:T(8,128)(2,1)S(1)}, bf16[1,128,2,256]{1,3,2,0:T(8,128)(2,1)S(1)}, u32[]{:S(2)}, u32[]{:S(2)}) collective-permute-start(bf16[1,128,2,256]{1,3,2,0:T(8,128)(2,1)S(1)} %get-tuple-element.44), channel_id=1, source_target_pairs={{2,0},{4,2},{6,4},{8,6},{10,8},{12,10},{14,12},{16,14},{18,16},{20... | collective-permute-start | bytes 393224 | tf_op jit(solution)/shard_map/ppermute | solution.py:25
  34.2 1.0 copy-start.2
  35.5 10.5 %copy-start.16 = (bf16[1,128,1,256]{1,3,2,0:T(8,128)(2,1)S(1)}, bf16[1,128,1,256]{1,3,2,0:T(8,128)(2,1)}, u32[]{:S(2)}) copy-start(bf16[1,128,1,256]{1,3,2,0:T(8,128)(2,1)} %copy-done.15) | copy-start | bytes 196612
  36.2 11.4 %collective-permute-start.6 = (bf16[1,128,1,256]{1,3,2,0:T(8,128)(2,1)S(1)}, bf16[1,128,1,256]{1,3,2,0:T(8,128)(2,1)S(1)}, u32[]{:S(2)}, u32[]{:S(2)}) collective-permute-start(bf16[1,128,1,256]{1,3,2,0:T(8,128)(2,1)S(1)} %get-tuple-element.37), channel_id=1, source_target_pairs={{0,2},{2,4},{4,6},{6,8},{8,10},{10,12},{12,14},{14,16},{16,18},{18... | collective-permute-start | bytes 196616 | tf_op jit(solution)/shard_map/ppermute | solution.py:22
  37.9 9.7 %collective-permute-start.7 = (bf16[1,128,1,256]{1,3,2,0:T(8,128)(2,1)S(1)}, bf16[1,128,1,256]{1,3,2,0:T(8,128)(2,1)S(1)}, u32[]{:S(2)}, u32[]{:S(2)}) collective-permute-start(bf16[1,128,1,256]{1,3,2,0:T(8,128)(2,1)S(1)} %get-tuple-element.38), channel_id=1, source_target_pairs={{2,0},{4,2},{6,4},{8,6},{10,8},{12,10},{14,12},{16,14},{18,16},{20... | collective-permute-start | bytes 196616 | tf_op jit(solution)/shard_map/ppermute | solution.py:25
  41.7 52.0 %collective-permute-start.2 = (bf16[1,128,2,256]{1,3,2,0:T(8,128)(2,1)S(1)}, bf16[1,128,2,256]{1,3,2,0:T(8,128)(2,1)S(1)}, u32[]{:S(2)}, u32[]{:S(2)}) collective-permute-start(bf16[1,128,2,256]{1,3,2,0:T(8,128)(2,1)S(1)} %get-tuple-element.39), channel_id=1, source_target_pairs={{0,2},{2,4},{4,6},{6,8},{8,10},{10,12},{12,14},{14,16},{16,18},{18... | collective-permute-start | bytes 393224 | tf_op jit(solution)/shard_map/ppermute | solution.py:22
  41.7 52.0 %collective-permute-start.3 = (bf16[1,128,2,256]{1,3,2,0:T(8,128)(2,1)S(1)}, bf16[1,128,2,256]{1,3,2,0:T(8,128)(2,1)S(1)}, u32[]{:S(2)}, u32[]{:S(2)}) collective-permute-start(bf16[1,128,2,256]{1,3,2,0:T(8,128)(2,1)S(1)} %get-tuple-element.40), channel_id=1, source_target_pairs={{2,0},{4,2},{6,4},{8,6},{10,8},{12,10},{14,12},{16,14},{18,16},{20... | collective-permute-start | bytes 393224 | tf_op jit(solution)/shard_map/ppermute | solution.py:25
  50.4 2.2 copy-start.21
  102.4 2.3 copy-start.14
  103.7 1.4 copy-start.6
  103.7 1.4 copy-start.7
  103.7 1.4 copy-start.12
  104.7 226.2 %all-reduce.9.cloned.1.call-start = ((), (), s32[]{:S(2)}) async-start(), calls=%async_computation.1 | async-start | bytes 2359296 | tf_op jit(solution)/shard_map/psum | solution.py:175
  107.1 11.8 %copy-start.9 = (bf16[2,128,128]{2,1,0:T(8,128)(2,1)S(1)}, bf16[2,128,128]{2,1,0:T(8,128)(2,1)}, u32[]{:S(2)}) copy-start(bf16[2,128,128]{2,1,0:T(8,128)(2,1)} %all_gather.7) | copy-start | bytes 196612
  330.9 2.0 copy-start.3
  (9 other events, 7.2 us)
Sparse Core Ops, SparseCore 0:
  104.8 87.5 all-reduce.6
  199.4 131.4 all-reduce.8
where the time goes:
time: 343 us; the launch traced here: 341 us
  waiting for transfers between devices  209 us (61%)
  blocking collectives  55.5 us (16%)
  matrix products  19.5 us (6%)
  starting transfers between devices  15.7 us (5%)
  other arithmetic  15.1 us (4%)
  between operations  14.6 us (4%)
  local copies, waits for them, and re-layouts  11 us (3%)
    psum x1, waiting for transfers between devices, shards(): lax.psum((second_kernel_partial, first_kernel_partial, input_local, embed...  137 us
    psum x1, waiting for transfers between devices, shards(): join_total = lax.psum(join_local, 'az')  72.1 us
    psum x1, blocking collectives, shards(): lax.psum((second_kernel_partial, first_kernel_partial, input_local, embed...  40.2 us
    all_gather x1, blocking collectives, shards(): lax.all_gather(final_state[None], 'el', axis=0, tiled=True)  11.6 us
    ppermute x4, starting transfers between devices, padded_2(): lax.ppermute(lax.slice_in_dim(block, 0, width, axis=dim), axis, backward)  9.38 us
    dot_general x18, matrix products, kernel_gradient_of(): jnp.einsum('niar,noar->io', window, upstream, preferred_element_type=jnp....  8.69 us
  transfers between devices with their start and end apart: 10, of which 2 were waited for; matrix products, arithmetic and copies ran while one was open for 5% of the time, Pallas kernels for 0%

commit v1 on v0

v1 whole, which is shorter than its diff:
```python
import functools
import math

import jax
import jax.numpy as jnp
from jax import lax
from jax.experimental import pallas as pl
from jax.experimental.pallas import tpu as pltpu
from jax.sharding import PartitionSpec as P

C = 128
D1 = 1
D2 = 2
HALO = D1 + D2
BF = jnp.bfloat16
F32 = jnp.float32
MESH = pl.DeviceIdType.MESH
NN = (((1,), (0,)), ((), ()))
NT = (((1,), (1,)), ((), ()))
TN = (((0,), (0,)), ((), ()))


def dot(a, b, dims):
    return lax.dot_general(a, b, dims, preferred_element_type=F32)


def up8(n):
    return -(-n // 8) * 8


def logistic(v):
    return 1.0 / (1.0 + jnp.exp(-v))


def slope(v):
    s = logistic(v)
    return s * (1.0 + v * (1.0 - s))


def layout(sweeps, naz):
    rows = 2 * 9 * C + 24 + up8(sweeps)
    share = up8(-(-rows // naz))
    own = C // naz
    chunk = -(-(share + own) // 16) * 16
    share = chunk - own
    return share, own, chunk


def pieces(start, count, share, chunk):
    out = []
    done = 0
    while done < count:
        k, off = divmod(start + done, share)
        size = min(count - done, share - off)
        out.append((done, k * chunk + off, size))
        done += size
    return out


def fill_taps(ref, value, dilate, gates):
    n = value.shape[1]
    gate = lax.broadcasted_iota(jnp.int32, value.shape, 1) % gates
    low = jnp.where(gate >= dilate, pltpu.roll(value, dilate, 1), 0.0)
    high = jnp.where(gate < gates - dilate, pltpu.roll(value, n - dilate, 1), 0.0)
    ref[0:C, :] = low.astype(BF)
    ref[C : 2 * C, :] = value.astype(BF)
    ref[2 * C : 3 * C, :] = high.astype(BF)


def compute_kernel(
    share, own, chunk, naz, gates, rays, scale,
    ids_ref, xc_ref, embed_ref, proj_ref, k1_ref, k2_ref, wj_ref, head_ref,
    pred_ref, pay_ref,
    t0, t1, tu2, tu1, pack,
):
    g = gates
    n = rays * g
    nx = xc_ref.shape[1]
    sweeps = embed_ref.shape[0]
    slots = ids_ref.shape[0]

    def put(start, value):
        for src, dst, size in pieces(start, value.shape[0], share, chunk):
            pack[dst : dst + size, :] = value[src : src + size, :]

    def conv(k_ref, taps, first, step, width):
        total = None
        for p in range(3):
            kp = k_ref[p * 3 * C : (p + 1) * 3 * C, :]
            term = dot(kp, taps[:, first + p * step : first + p * step + width], TN)
            total = term if total is None else total + term
        return total

    def back(k_ref, taps, step, width):
        total = None
        for p in range(3):
            m = jnp.concatenate(
                [
                    k_ref[((2 - p) * 3 + 2 - q) * C : ((2 - p) * 3 + 3 - q) * C, :]
                    for q in range(3)
                ],
                axis=1,
            )
            term = dot(m, taps[:, p * step : p * step + width], NN)
            total = term if total is None else total + term
        return total

    pack[...] = jnp.zeros_like(pack)
    owns = []
    row = jnp.zeros((1, C), F32)
    for s in range(sweeps):
        w = jnp.float32(0.0)
        for j in range(slots):
            w = w + jnp.where(ids_ref[j] == s, 1.0, 0.0)
        owns.append(w)
        row = row + w * embed_ref[s : s + 1, :]
    bias = jnp.broadcast_to(row, (C, C)).T[:, 0:1]

    s0 = (dot(proj_ref[...], xc_ref[0:48, :], TN) + bias).astype(BF).astype(F32)
    fill_taps(t0, s0 * logistic(s0), D1, g)

    w1 = (rays + 2 * D2) * g
    s1 = s0[:, D1 * g : D1 * g + w1] + conv(k1_ref, t0, 0, D1 * g, w1)
    s1 = s1.astype(BF).astype(F32)
    fill_taps(t1, s1 * logistic(s1), D2, g)
    s2 = s1[:, D2 * g : D2 * g + n] + conv(k2_ref, t1, 0, D2 * g, n)
    s2 = s2.astype(BF)

    joined = dot(wj_ref[...], s2, TN).astype(BF)
    pred_ref[...] = dot(head_ref[...], joined, NN)

    jb = dot(head_ref[...], xc_ref[48:64, :], TN).astype(BF)
    join = dot(s2, jb[:, HALO * g : HALO * g + n], NT) * scale
    for k in range(naz):
        pack[k * chunk + share : (k + 1) * chunk, :] = join[k * own : (k + 1) * own, :]

    g2 = dot(wj_ref[...], jb, NN)
    fill_taps(tu2, g2, D2, g)
    for p in range(3):
        part = dot(
            t1[:, p * D2 * g : p * D2 * g + n], tu2[C : 2 * C, HALO * g : HALO * g + n], NT
        )
        put((3 + p) * 3 * C, part * scale)

    wb = (rays + 2 * D1) * g
    g1 = g2[:, D2 * g : D2 * g + wb] + back(k2_ref, tu2, D2 * g, wb) * slope(
        s1[:, (D2 - D1) * g : (D2 - D1) * g + wb]
    )
    fill_taps(tu1, g1, D1, g)
    for p in range(3):
        first = (HALO + D1 * (p - 1)) * g
        part = dot(t0[:, first : first + n], tu1[C : 2 * C, D1 * g : D1 * g + n], NT)
        put(p * 3 * C, part * scale)
    g0 = g1[:, D1 * g : D1 * g + n] + back(k1_ref, tu1, D1 * g, n) * slope(
        s0[:, HALO * g : HALO * g + n]
    )
    g0 = g0.astype(BF)
    gin = dot(xc_ref[0:48, HALO * g : HALO * g + n], g0, NT)
    put(18 * C, (gin[0:24, :] + gin[24:48, :]) * scale)
    column = dot(jnp.ones((8, n), BF), g0, NT)[0:1, :] * scale
    lines = up8(sweeps)
    index = lax.broadcasted_iota(jnp.int32, (lines, C), 0)
    grads = jnp.zeros((lines, C), F32)
    for s in range(sweeps):
        grads = grads + jnp.where(index == s, owns[s] * column, 0.0)
    put(18 * C + 24, grads)
    pay_ref[...] = pack[...].astype(BF)


def sum_kernel(
    share, own, chunk, naz, nel,
    pred_in, pay,
    pred_out, join_out, first_out, second_out, input_out, embed_out,
    rbuf, mbuf, gbuf, pbuf,
    s1, r1, s2, r2, s3, r3, sp, rp,
):
    a = lax.axis_index("az")
    e = lax.axis_index("el")
    barrier = pltpu.get_barrier_semaphore()
    for s in range(1, naz):
        pl.semaphore_signal(
            barrier, inc=1, device_id={"az": lax.rem(a + s, naz), "el": e}, device_id_type=MESH
        )
    for t in range(1, nel):
        pl.semaphore_signal(
            barrier, inc=1, device_id={"az": a, "el": lax.rem(e + t, nel)}, device_id_type=MESH
        )
    pl.semaphore_wait(barrier, naz + nel - 2)

    scatter = []
    for s in range(1, naz):
        d = lax.rem(a + s, naz)
        c = pltpu.make_async_remote_copy(
            src_ref=pay.at[pl.ds(pl.multiple_of(d * chunk, 16), chunk), :],
            dst_ref=rbuf.at[s],
            send_sem=s1.at[s],
            recv_sem=r1.at[s],
            device_id={"az": d, "el": e},
            device_id_type=MESH,
        )
        c.start()
        scatter.append(c)
    sends = []
    for t in range(1, nel):
        c = pltpu.make_async_remote_copy(
            src_ref=pred_in,
            dst_ref=pbuf.at[e],
            send_sem=sp.at[t],
            recv_sem=rp.at[t],
            device_id={"az": a, "el": lax.rem(e + t, nel)},
            device_id_type=MESH,
        )
        c.start()
        sends.append(c)
    pbuf[e] = pred_in[...]
    mine = pl.ds(pl.multiple_of(a * chunk, 16), chunk)
    acc = pay[mine, :].astype(F32)
    for s in range(1, naz):
        scatter[s - 1].wait_recv()
        acc = acc + rbuf[s].astype(F32)
    mbuf[e] = acc.astype(BF)
    cross = []
    for t in range(1, nel):
        c = pltpu.make_async_remote_copy(
            src_ref=mbuf.at[e],
            dst_ref=mbuf.at[e],
            send_sem=s2.at[t],
            recv_sem=r2.at[t],
            device_id={"az": a, "el": lax.rem(e + t, nel)},
            device_id_type=MESH,
        )
        c.start()
        cross.append(c)
    for c in cross:
        c.wait_recv()
    total = mbuf[0].astype(F32)
    for t in range(1, nel):
        total = total + mbuf[t].astype(F32)
    line = lax.broadcasted_iota(jnp.int32, total.shape, 0)
    total = jnp.where(line < share, total, acc)
    gbuf[mine, :] = total.astype(BF)
    gather = []
    for s in range(1, naz):
        c = pltpu.make_async_remote_copy(
            src_ref=gbuf.at[mine, :],
            dst_ref=gbuf.at[mine, :],
            send_sem=s3.at[s],
            recv_sem=r3.at[s],
            device_id={"az": lax.rem(a + s, naz), "el": e},
            device_id_type=MESH,
        )
        c.start()
        gather.append(c)
    for c in sends:
        c.wait_recv()
    leads = pred_out.shape[0]
    pred = pbuf[0]
    for t in range(1, nel):
        pred = pred + pbuf[t]
    pred_out[...] = pred[0:leads, :]
    for c in gather:
        c.wait_recv()

    def take(ref, start):
        for dst, src, size in pieces(start, ref.shape[0], share, chunk):
            ref[dst : dst + size, :] = gbuf[src : src + size, :].astype(F32)

    take(first_out, 0)
    take(second_out, 9 * C)
    take(input_out, 18 * C)
    take(embed_out, 18 * C + 24)
    for k in range(naz):
        join_out[k * own : (k + 1) * own, :] = gbuf[
            k * chunk + share : (k + 1) * chunk, :
        ].astype(F32)
    for c in scatter + sends + cross + gather:
        c.wait_send()


def shards(
    raw_sweeps, sweep_ids, elevation_embed, input_proj, first_kernel, second_kernel,
    join_weight, head_weight, cotangent,
):
    naz = lax.axis_size("az")
    nel = lax.axis_size("el")
    slots, _, inputs, rays, gates = raw_sweeps.shape
    leads = head_weight.shape[0]
    sweeps = elevation_embed.shape[0]
    share, own, chunk = layout(sweeps, naz)
    scale = 1.0 / math.sqrt(nel * rays * naz * gates)
    n = rays * gates
    h = HALO * gates

    xc = jnp.concatenate(
        [
            raw_sweeps.reshape(slots * inputs, n),
            cotangent.reshape(leads, n),
            jnp.zeros((16 - leads, n), BF),
        ],
        axis=0,
    )
    forward = [(i, (i + 1) % naz) for i in range(naz)]
    backward = [(t, s) for s, t in forward]
    low = lax.ppermute(xc[:, n - h :], "az", forward)
    high = lax.ppermute(xc[:, :h], "az", backward)
    xc = jnp.concatenate([low, xc, high], axis=1)
    proj = jnp.concatenate([input_proj] * slots, axis=0)
    head = jnp.pad(head_weight, ((0, 16 - leads), (0, 0)))
    vm = pl.BlockSpec(memory_space=pltpu.VMEM)
    total = naz * chunk
    pred, pay = pl.pallas_call(
        functools.partial(compute_kernel, share, own, chunk, naz, gates, rays, scale),
        out_shape=(
            jax.ShapeDtypeStruct((16, n), F32),
            jax.ShapeDtypeStruct((total, C), BF),
        ),
        in_specs=[pl.BlockSpec(memory_space=pltpu.SMEM)] + [vm] * 7,
        out_specs=(vm, vm),
        scratch_shapes=[
            pltpu.VMEM((3 * C, n + 2 * h), BF),
            pltpu.VMEM((3 * C, (rays + 2 * D2) * gates), BF),
            pltpu.VMEM((3 * C, n + 2 * h), BF),
            pltpu.VMEM((3 * C, (rays + 2 * D1) * gates), BF),
            pltpu.VMEM((total, C), F32),
        ],
        compiler_params=pltpu.CompilerParams(vmem_limit_bytes=48 * 1024 * 1024),
        name="step_compute",
    )(
        sweep_ids, xc, elevation_embed, proj,
        first_kernel.reshape(9 * C, C), second_kernel.reshape(9 * C, C),
        join_weight[0], head,
    )
    dma = pltpu.SemaphoreType.DMA
    pred, join, first, second, gin, emb = pl.pallas_call(
        functools.partial(sum_kernel, share, own, chunk, naz, nel),
        out_shape=(
            jax.ShapeDtypeStruct((leads, n), F32),
            jax.ShapeDtypeStruct((C, C), F32),
            jax.ShapeDtypeStruct((9 * C, C), F32),
            jax.ShapeDtypeStruct((9 * C, C), F32),
            jax.ShapeDtypeStruct((inputs, C), F32),
            jax.ShapeDtypeStruct((sweeps, C), F32),
        ),
        in_specs=[vm, vm],
        out_specs=(vm,) * 6,
        scratch_shapes=[
            pltpu.VMEM((naz, chunk, C), BF),
            pltpu.VMEM((nel, chunk, C), BF),
            pltpu.VMEM((total, C), BF),
            pltpu.VMEM((nel, 16, n), F32),
            dma((naz,)), dma((naz,)), dma((nel,)), dma((nel,)),
            dma((naz,)), dma((naz,)), dma((nel,)), dma((nel,)),
        ],
        compiler_params=pltpu.CompilerParams(collective_id=0, has_side_effects=True),
        name="step_sum",
    )(pred, pay)
    shape = first_kernel.shape
    return (
        pred.reshape(1, leads, rays, gates),
        join[None],
        first.reshape(shape),
        second.reshape(shape),
        gin,
        emb,
    )


def solution(mesh):
    in_specs = (
        P("el", None, None, "az", None),
        P("el"),
        P(),
        P(),
        P(),
        P(),
        P("el", None, None),
        P(),
        P(None, None, "az", None),
    )
    out_specs = (P(None, None, "az", None), P("el", None, None), P(), P(), P(), P())
    return jax.shard_map(shards, mesh=mesh, in_specs=in_specs, out_specs=out_specs, check_vma=False)
```

time: 343 us -> 67.2 us (0.20)
  the two profiles are of different devices: /device:TPU:1 before, /device:TPU:27 now
where the time goes in v1:
time: 67.2 us; the launch traced here: 66.9 us
  Pallas kernels  49.7 us (74%)
  local copies, waits for them, and re-layouts  9.53 us (14%)
  waiting for transfers between devices  6 us (9%)
  between operations  0.81 us (1%)
  starting transfers between devices  0.79 us (1%)
    pallas_call x1, Pallas kernels, shards(): pl.pallas_call(functools.partial(sum_kernel, share, own, chunk, naz, nel)...  40.5 us
    pallas_call x1, Pallas kernels, shards(): pl.pallas_call(functools.partial(compute_kernel, share, own, chunk, naz,...  9.24 us
    unnamed x37, local copies, waits for them, and re-layouts  7.85 us
    ppermute x1, waiting for transfers between devices, shards(): high = lax.ppermute(xc[:, :h], 'az', backward)  5.16 us
    reshape x1, local copies, waits for them, and re-layouts, shards(): pred.reshape(1, leads, rays, gates)  1.64 us
  transfers between devices with their start and end apart: 2, of which 2 were waited for; matrix products, arithmetic and copies ran while one was open for 0% of the time, Pallas kernels for 0%

profile of v1, /device:TPU:27, one launch (start us, length us, event | category | flops | bytes accessed | tf_op | source)
XLA Modules:
  0.0 66.9 jit_solution(8645615672437252872)
XLA Ops:
  0.6 0.8 %pad.15 = bf16[16,6,256]{2,1,0:T(8,128)(2,1)S(1)} pad(bf16[12,6,256]{2,1,0:T(8,128)(2,1)} %bitcast.26, bf16[]{:T(256)} %constant.1.clone.1), padding=0_4x0_0x0_0 | pad | bytes 86018
  1.5 0.1 copy-done.8
  1.7 0.0 copy-start.12
  1.7 0.0 copy-start.11
  1.7 0.1 collective-permute-start
  1.8 0.7 %collective-permute-start.1 = (bf16[64,768]{1,0:T(8,128)(2,1)S(1)}, bf16[64,768]{1,0:T(8,128)(2,1)S(1)}, u32[]{:S(2)}, u32[]{:S(2)}) collective-permute-start(bf16[64,768]{1,0:T(8,128)(2,1)S(1)} %get-tuple-element.35), channel_id=1, source_target_pairs={{2,0},{4,2},{6,4},{8,6},{10,8},{12,10},{14,12},{16,14},{18,16},{20... | collective-permute-start | bytes 294920 | tf_op jit(solution)/shard_map/ppermute | solution.py:305
  2.6 0.0 copy-start.1
  2.6 0.0 copy-start.2
  2.6 0.0 copy-start.4
  2.6 0.8 %collective-permute-done = bf16[64,768]{1,0:T(8,128)(2,1)S(1)} collective-permute-done((bf16[64,768]{1,0:T(8,128)(2,1)S(1)}, bf16[64,768]{1,0:T(8,128)(2,1)S(1)}, u32[]{:S(2)}, u32[]{:S(2)}) %collective-permute-start) | collective-permute-done | bytes 98336 | tf_op jit(solution)/shard_map/ppermute | solution.py:304
  3.4 5.2 %collective-permute-done.1 = bf16[64,768]{1,0:T(8,128)(2,1)S(1)} collective-permute-done((bf16[64,768]{1,0:T(8,128)(2,1)S(1)}, bf16[64,768]{1,0:T(8,128)(2,1)S(1)}, u32[]{:S(2)}, u32[]{:S(2)}) %collective-permute-start.1) | collective-permute-done | bytes 98336 | tf_op jit(solution)/shard_map/ppermute | solution.py:305
  8.6 0.0 copy-start.6
  8.7 0.6 copy-done.5
  9.3 9.2 %step_compute.1 = (f32[16,1536]{1,0:T(8,128)S(1)}, bf16[2560,128]{1,0:T(8,128)(2,1)S(1)}) custom-call(s32[2]{0:T(128)S(1)} %copy-done.6, bf16[64,3072]{1,0:T(8,128)(2,1)S(1)} %pad_maximum_fusion.xc_ref, f32[4,128]{1,0:T(4,128)S(1)} %copy-done.5, bf16[48,128]{1,0:T(8,128)(2,1)S(1)} %pad_maximum_fusion.2.proj_ref, bf16[1152,128]{1,0:T(8,128)(2,1)S(1)} %bitcast.14, ...), custom_call_target="tpu_custom_call" | custom-call | tf_op jit(solution)/shard_map/step_compute/pallas_call | solution.py:311
  18.6 0.9 %copy-done = bf16[2560,128]{1,0:T(8,128)(2,1)} copy-done((bf16[2560,128]{1,0:T(8,128)(2,1)}, bf16[2560,128]{1,0:T(8,128)(2,1)S(1)}, u32[]{:S(2)}) %copy-start) | copy-done | bytes 655384
  19.4 0.6 copy-done.3
  20.1 40.5 %step_sum.1 = (f32[12,1536]{1,0:T(8,128)}, f32[128,128]{1,0:T(8,128)}, f32[1152,128]{1,0:T(8,128)}, f32[1152,128]{1,0:T(8,128)}, f32[24,128]{1,0:T(8,128)}, /*index=5*/f32[4,128]{1,0:T(4,128)}) custom-call(f32[16,1536]{1,0:T(8,128)} %copy-done.3, bf16[2560,128]{1,0:T(8,128)(2,1)} %copy-done), custom_call_target="tpu_custom_call" | custom-call | tf_op jit(solution)/shard_map/step_sum/pallas_call | solution.py:334
  60.6 1.6 %reshape.40 = f32[1,12,6,256]{3,0,2,1:T(1,128)} reshape(f32[12,1536]{1,0:T(8,128)} %get-tuple-element.16) | data formatting | bytes 147456 | tf_op jit(solution)/shard_map/reshape | solution.py:359
  62.2 0.6 copy.26
  62.8 2.0 %copy.27 = f32[3,3,128,128]{3,2,1,0:T(8,128)} copy(f32[3,3,128,128]{3,2,1,0:T(8,128)} %bitcast.21) | data formatting | bytes 1179648
  64.8 0.8 %copy.28 = f32[3,3,128,128]{3,2,1,0:T(8,128)} copy(f32[3,3,128,128]{3,2,1,0:T(8,128)S(1)} %bitcast.20) | data formatting | bytes 1179648
  65.6 0.6 copy.29
  66.2 0.1 copy-done.13
  66.3 0.6 copy.30
  (26 shorter events, 0.2 us)
Async XLA Ops:
  0.6 0.9 %copy-start.8 = (bf16[2,1,24,6,256]{4,2,3,1,0:T(8,128)(2,1)S(1)}, bf16[2,1,24,6,256]{4,2,3,1,0:T(8,128)(2,1)}, u32[]{:S(2)}) copy-start(bf16[2,1,24,6,256]{4,2,3,1,0:T(8,128)(2,1)} %param.9) | copy-start | bytes 442372
  1.7 0.8 %copy-start.12 = (bf16[12,128]{1,0:T(8,128)(2,1)S(1)}, bf16[12,128]{1,0:T(8,128)(2,1)}, u32[]{:S(2)}) copy-start(bf16[12,128]{1,0:T(8,128)(2,1)} %param.16) | copy-start | bytes 9220
  1.7 0.8 %copy-start.11 = (bf16[24,128]{1,0:T(8,128)(2,1)S(1)}, bf16[24,128]{1,0:T(8,128)(2,1)}, u32[]{:S(2)}) copy-start(bf16[24,128]{1,0:T(8,128)(2,1)} %param.12) | copy-start | bytes 18436
  1.7 1.7 %collective-permute-start = (bf16[64,768]{1,0:T(8,128)(2,1)S(1)}, bf16[64,768]{1,0:T(8,128)(2,1)S(1)}, u32[]{:S(2)}, u32[]{:S(2)}) collective-permute-start(bf16[64,768]{1,0:T(8,128)(2,1)S(1)} %get-tuple-element.34), channel_id=1, source_target_pairs={{0,2},{2,4},{4,6},{6,8},{8,10},{10,12},{12,14},{14,16},{16,18},{18... | collective-permute-start | bytes 294920 | tf_op jit(solution)/shard_map/ppermute | solution.py:304
  1.8 6.8 %collective-permute-start.1 = (bf16[64,768]{1,0:T(8,128)(2,1)S(1)}, bf16[64,768]{1,0:T(8,128)(2,1)S(1)}, u32[]{:S(2)}, u32[]{:S(2)}) collective-permute-start(bf16[64,768]{1,0:T(8,128)(2,1)S(1)} %get-tuple-element.35), channel_id=1, source_target_pairs={{2,0},{4,2},{6,4},{8,6},{10,8},{12,10},{14,12},{16,14},{18,16},{20... | collective-permute-start | bytes 294920 | tf_op jit(solution)/shard_map/ppermute | solution.py:305
  2.6 6.1 %copy-start.1 = (bf16[3,3,128,128]{3,2,1,0:T(8,128)(2,1)S(1)}, bf16[3,3,128,128]{3,2,1,0:T(8,128)(2,1)}, u32[]{:S(2)}) copy-start(bf16[3,3,128,128]{3,2,1,0:T(8,128)(2,1)} %param.13) | copy-start | bytes 884740
  2.6 6.1 %copy-start.2 = (bf16[3,3,128,128]{3,2,1,0:T(8,128)(2,1)S(1)}, bf16[3,3,128,128]{3,2,1,0:T(8,128)(2,1)}, u32[]{:S(2)}) copy-start(bf16[3,3,128,128]{3,2,1,0:T(8,128)(2,1)} %param.14) | copy-start | bytes 884740
  2.6 6.1 %copy-start.4 = (bf16[1,128,128]{2,1,0:T(8,128)(2,1)S(1)}, bf16[1,128,128]{2,1,0:T(8,128)(2,1)}, u32[]{:S(2)}) copy-start(bf16[1,128,128]{2,1,0:T(8,128)(2,1)} %param.15) | copy-start | bytes 98308
  8.6 0.7 %copy-start.5 = (f32[4,128]{1,0:T(4,128)S(1)}, f32[4,128]{1,0:T(4,128)}, u32[]{:S(2)}) copy-start(f32[4,128]{1,0:T(4,128)} %embed_ref.1) | copy-start | bytes 6148
  8.6 0.7 %copy-start.6 = (s32[2]{0:T(128)S(1)}, s32[2]{0:T(128)}, u32[]{:S(2)}) copy-start(s32[2]{0:T(128)} %ids_ref.1) | copy-start | bytes 28
  18.6 0.9 %copy-start = (bf16[2560,128]{1,0:T(8,128)(2,1)}, bf16[2560,128]{1,0:T(8,128)(2,1)S(1)}, u32[]{:S(2)}) copy-start(bf16[2560,128]{1,0:T(8,128)(2,1)S(1)} %get-tuple-element.15.pay) | copy-start | bytes 1966084
  19.4 0.6 copy-start.3
  60.6 1.7 %copy-start.9 = (f32[128,128]{1,0:T(8,128)S(1)}, f32[128,128]{1,0:T(8,128)}, u32[]{:S(2)}) copy-start(f32[128,128]{1,0:T(8,128)} %get-tuple-element.17) | copy-start | bytes 196612
  62.8 2.0 %copy-start.7 = (f32[1152,128]{1,0:T(8,128)S(1)}, f32[1152,128]{1,0:T(8,128)}, u32[]{:S(2)}) copy-start(f32[1152,128]{1,0:T(8,128)} %get-tuple-element.19) | copy-start | bytes 1769476
  64.8 0.8 %copy-start.10 = (f32[24,128]{1,0:T(8,128)S(1)}, f32[24,128]{1,0:T(8,128)}, u32[]{:S(2)}) copy-start(f32[24,128]{1,0:T(8,128)} %get-tuple-element.46) | copy-start | bytes 36868
  65.6 0.7 %copy-start.13 = (f32[4,128]{1,0:T(4,128)S(1)}, f32[4,128]{1,0:T(4,128)}, u32[]{:S(2)}) copy-start(f32[4,128]{1,0:T(4,128)} %get-tuple-element.47) | copy-start | bytes 6148

commit v2 on v1

v2 whole, which is shorter than its diff:
```python
import functools
import math

import jax
import jax.numpy as jnp
from jax import lax
from jax.experimental import pallas as pl
from jax.experimental.pallas import tpu as pltpu
from jax.sharding import PartitionSpec as P

C = 128
D1 = 1
D2 = 2
HALO = D1 + D2
BF = jnp.bfloat16
F32 = jnp.float32
MESH = pl.DeviceIdType.MESH
NN = (((1,), (0,)), ((), ()))
NT = (((1,), (1,)), ((), ()))
TN = (((0,), (0,)), ((), ()))


def dot(a, b, dims):
    return lax.dot_general(a, b, dims, preferred_element_type=F32)


def up8(n):
    return -(-n // 8) * 8


def up16(n):
    return -(-n // 16) * 16


def logistic(v):
    return 1.0 / (1.0 + jnp.exp(-v))


def slope(v):
    s = logistic(v)
    return s * (1.0 + v * (1.0 - s))


def layouts(sweeps, naz):
    own = C // naz
    share = up8(-(-9 * C // naz))
    chunk = up16(share + own)
    rest = up16(-(-(9 * C + 24 + up8(sweeps)) // naz))
    return (chunk - own, own, chunk), (rest, 0, rest)


def pieces(start, count, share, chunk):
    out = []
    done = 0
    while done < count:
        k, off = divmod(start + done, share)
        size = min(count - done, share - off)
        out.append((done, k * chunk + off, size))
        done += size
    return out


def fill_taps(ref, value, dilate, gates):
    n = value.shape[1]
    gate = lax.broadcasted_iota(jnp.int32, value.shape, 1) % gates
    low = jnp.where(gate >= dilate, pltpu.roll(value, dilate, 1), 0.0)
    high = jnp.where(gate < gates - dilate, pltpu.roll(value, n - dilate, 1), 0.0)
    ref[0:C, :] = low.astype(BF)
    ref[C : 2 * C, :] = value.astype(BF)
    ref[2 * C : 3 * C, :] = high.astype(BF)


def step_kernel(
    parts, naz, nel, gates, rays, scale,
    ids_ref, xc_ref, embed_ref, proj_ref, k1_ref, k2_ref, wj_ref, head_ref,
    pred_out, join_out, first_out, second_out, input_out, embed_out,
    xe, t0, t1, tu2, tu1,
    pack0, pack1, pay0, pay1, abuf0, abuf1, half0, half1,
    rbuf0, rbuf1, mbuf0, mbuf1, gbuf0, gbuf1, pbuf,
    sh, rh, sa, ra, sb, rb, sc, rc, sd, rd, se, re, sp, rp,
):
    packs, pays, abufs, halves = (pack0, pack1), (pay0, pay1), (abuf0, abuf1), (half0, half1)
    rbufs, mbufs, gbufs = (rbuf0, rbuf1), (mbuf0, mbuf1), (gbuf0, gbuf1)
    g = gates
    n = rays * g
    h = HALO * g
    sweeps = embed_ref.shape[0]
    slots = ids_ref.shape[0]
    nq = naz // 2
    a = lax.axis_index("az")
    e = lax.axis_index("el")
    core = lax.rem(a, 2)
    q = a // 2
    started = []

    def at(az, el):
        return {"az": az, "el": el}

    partner = at(a + 1 - 2 * core, e)
    right = at(lax.rem(a + 1, naz), e)
    left = at(lax.rem(a + naz - 1, naz), e)
    same = [at(2 * lax.rem(q + s, nq) + core, e) for s in range(nq)]
    column = [at(a, lax.rem(e + t, nel)) for t in range(nel)]

    barrier = pltpu.get_barrier_semaphore()
    greeted = [partner, right, left] + same[1:] + column[1:]
    for device in greeted:
        pl.semaphore_signal(barrier, inc=1, device_id=device, device_id_type=MESH)
    xe[:, h : h + n] = xc_ref[...]
    pl.semaphore_wait(barrier, len(greeted))

    def send(source, target, ssem, rsem, device):
        c = pltpu.make_async_remote_copy(
            src_ref=source, dst_ref=target, send_sem=ssem, recv_sem=rsem,
            device_id=device, device_id_type=MESH,
        )
        c.start()
        started.append(c)
        return c

    up = send(xc_ref.at[:, n - h : n], xe.at[:, 0:h], sh.at[0], rh.at[0], right)
    down = send(xc_ref.at[:, 0:h], xe.at[:, h + n : n + 2 * h], sh.at[1], rh.at[1], left)

    def rows(index, chunk):
        return pl.ds(pl.multiple_of(index * chunk, 16), chunk)

    def put(i, start, value):
        share, own, chunk = parts[i]
        for src, dst, size in pieces(start, value.shape[0], share, chunk):
            packs[i][dst : dst + size, :] = value[src : src + size, :]

    def phase_a(i):
        chunk = parts[i][2]
        pays[i][...] = packs[i][...].astype(BF)
        return send(
            pays[i].at[rows(1 - core, nq * chunk), :], abufs[i], sa.at[i], ra.at[i], partner
        )

    def phase_b(i, arrived):
        chunk = parts[i][2]
        arrived.wait_recv()
        mine = pays[i][rows(core, nq * chunk), :].astype(F32)
        halves[i][...] = (mine + abufs[i][...].astype(F32)).astype(BF)
        return [
            send(
                halves[i].at[rows(lax.rem(q + s, nq), chunk), :], rbufs[i].at[s],
                sb.at[i, s], rb.at[i, s], same[s],
            )
            for s in range(1, nq)
        ]

    def phase_c(i, arrived):
        chunk = parts[i][2]
        acc = halves[i][rows(q, chunk), :].astype(F32)
        for s in range(1, nq):
            arrived[s - 1].wait_recv()
            acc = acc + rbufs[i][s].astype(F32)
        mbufs[i][e] = acc.astype(BF)
        sent = [
            send(mbufs[i].at[e], mbufs[i].at[e], sc.at[i, t], rc.at[i, t], column[t])
            for t in range(1, nel)
        ]
        return acc, sent

    def phase_d(i, acc, arrived):
        share, own, chunk = parts[i]
        for c in arrived:
            c.wait_recv()
        total = mbufs[i][0].astype(F32)
        for t in range(1, nel):
            total = total + mbufs[i][t].astype(F32)
        if own:
            line = lax.broadcasted_iota(jnp.int32, total.shape, 0)
            total = jnp.where(line < share, total, acc)
        mine = rows(core * nq + q, chunk)
        gbufs[i][mine, :] = total.astype(BF)
        view = gbufs[i].at[mine, :]
        sent = [send(view, view, sd.at[i, s], rd.at[i, s], same[s]) for s in range(1, nq)]
        own_sent = send(view, view, se.at[i, 0], re.at[i, 0], partner)
        return sent, own_sent

    def phase_e(i, arrived, own_sent):
        chunk = parts[i][2]
        last = [own_sent]
        for s in range(1, nq):
            arrived[s - 1].wait_recv()
            view = gbufs[i].at[rows(core * nq + lax.rem(q + nq - s, nq), chunk), :]
            last.append(send(view, view, se.at[i, s], re.at[i, s], partner))
        return last

    def take(i, ref, start):
        share, own, chunk = parts[i]
        for dst, src, size in pieces(start, ref.shape[0], share, chunk):
            ref[dst : dst + size, :] = gbufs[i][src : src + size, :].astype(F32)

    def conv(k_ref, taps, first, step, width):
        total = None
        for p in range(3):
            kp = k_ref[p * 3 * C : (p + 1) * 3 * C, :]
            term = dot(kp, taps[:, first + p * step : first + p * step + width], TN)
            total = term if total is None else total + term
        return total

    def back(k_ref, taps, step, width):
        total = None
        for p in range(3):
            m = jnp.concatenate(
                [
                    k_ref[((2 - p) * 3 + 2 - q_) * C : ((2 - p) * 3 + 3 - q_) * C, :]
                    for q_ in range(3)
                ],
                axis=1,
            )
            term = dot(m, taps[:, p * step : p * step + width], NN)
            total = term if total is None else total + term
        return total

    packs[0][...] = jnp.zeros_like(packs[0])
    packs[1][...] = jnp.zeros_like(packs[1])
    owns = []
    row = jnp.zeros((1, C), F32)
    for s in range(sweeps):
        w = jnp.float32(0.0)
        for j in range(slots):
            w = w + jnp.where(ids_ref[j] == s, 1.0, 0.0)
        owns.append(w)
        row = row + w * embed_ref[s : s + 1, :]
    bias = jnp.broadcast_to(row, (C, C)).T[:, 0:1]

    up.wait_recv()
    down.wait_recv()
    s0 = (dot(proj_ref[...], xe[0:48, :], TN) + bias).astype(BF).astype(F32)
    fill_taps(t0, s0 * logistic(s0), D1, g)

    w1 = (rays + 2 * D2) * g
    s1 = s0[:, D1 * g : D1 * g + w1] + conv(k1_ref, t0, 0, D1 * g, w1)
    s1 = s1.astype(BF).astype(F32)
    fill_taps(t1, s1 * logistic(s1), D2, g)
    s2 = s1[:, D2 * g : D2 * g + n] + conv(k2_ref, t1, 0, D2 * g, n)
    s2 = s2.astype(BF)

    jb = dot(head_ref[...], xe[48:64, :], TN).astype(BF)
    join = dot(s2, jb[:, HALO * g : HALO * g + n], NT) * scale
    share, own, chunk = parts[0]
    for k in range(naz):
        packs[0][k * chunk + share : (k + 1) * chunk, :] = join[k * own : (k + 1) * own, :]

    g2 = dot(wj_ref[...], jb, NN)
    fill_taps(tu2, g2, D2, g)
    for p in range(3):
        part = dot(
            t1[:, p * D2 * g : p * D2 * g + n], tu2[C : 2 * C, HALO * g : HALO * g + n], NT
        )
        put(0, p * 3 * C, part * scale)
    a0 = phase_a(0)

    joined = dot(wj_ref[...], s2, TN).astype(BF)
    pbuf[e] = dot(head_ref[...], joined, NN)

    wb = (rays + 2 * D1) * g
    g1 = g2[:, D2 * g : D2 * g + wb] + back(k2_ref, tu2, D2 * g, wb) * slope(
        s1[:, (D2 - D1) * g : (D2 - D1) * g + wb]
    )
    b0 = phase_b(0, a0)
    fill_taps(tu1, g1, D1, g)
    for p in range(3):
        first = (HALO + D1 * (p - 1)) * g
        part = dot(t0[:, first : first + n], tu1[C : 2 * C, D1 * g : D1 * g + n], NT)
        put(1, p * 3 * C, part * scale)
    g0 = g1[:, D1 * g : D1 * g + n] + back(k1_ref, tu1, D1 * g, n) * slope(
        s0[:, HALO * g : HALO * g + n]
    )
    g0 = g0.astype(BF)
    gin = dot(xe[0:48, HALO * g : HALO * g + n], g0, NT)
    put(1, 9 * C, (gin[0:24, :] + gin[24:48, :]) * scale)
    summed = dot(jnp.ones((8, n), BF), g0, NT)[0:1, :] * scale
    lines = up8(sweeps)
    index = lax.broadcasted_iota(jnp.int32, (lines, C), 0)
    grads = jnp.zeros((lines, C), F32)
    for s in range(sweeps):
        grads = grads + jnp.where(index == s, owns[s] * summed, 0.0)
    put(1, 9 * C + 24, grads)
    a1 = phase_a(1)
    acc0, c0 = phase_c(0, b0)
    b1 = phase_b(1, a1)
    d0, own0 = phase_d(0, acc0, c0)
    preds = [
        send(pbuf.at[e], pbuf.at[e], sp.at[t], rp.at[t], column[t]) for t in range(1, nel)
    ]
    acc1, c1 = phase_c(1, b1)
    d1, own1 = phase_d(1, acc1, c1)
    e0 = phase_e(0, d0, own0)
    for c in preds:
        c.wait_recv()
    pred = pbuf[0]
    for t in range(1, nel):
        pred = pred + pbuf[t]
    pred_out[...] = pred[0 : pred_out.shape[0], :]
    for c in e0:
        c.wait_recv()
    take(0, second_out, 0)
    for k in range(naz):
        join_out[k * own : (k + 1) * own, :] = gbufs[0][
            k * chunk + share : (k + 1) * chunk, :
        ].astype(F32)
    e1 = phase_e(1, d1, own1)
    for c in e1:
        c.wait_recv()
    take(1, first_out, 0)
    take(1, input_out, 9 * C)
    take(1, embed_out, 9 * C + 24)
    for c in started:
        c.wait_send()


def shards(
    raw_sweeps, sweep_ids, elevation_embed, input_proj, first_kernel, second_kernel,
    join_weight, head_weight, cotangent,
):
    naz = lax.axis_size("az")
    nel = lax.axis_size("el")
    slots, _, inputs, rays, gates = raw_sweeps.shape
    leads = head_weight.shape[0]
    sweeps = elevation_embed.shape[0]
    parts = layouts(sweeps, naz)
    scale = 1.0 / math.sqrt(nel * rays * naz * gates)
    n = rays * gates
    h = HALO * gates
    nq = naz // 2

    xc = jnp.concatenate(
        [
            raw_sweeps.reshape(slots * inputs, n),
            cotangent.reshape(leads, n),
            jnp.zeros((16 - leads, n), BF),
        ],
        axis=0,
    )
    proj = jnp.concatenate([input_proj] * slots, axis=0)
    head = jnp.pad(head_weight, ((0, 16 - leads), (0, 0)))
    vm = pl.BlockSpec(memory_space=pltpu.VMEM)
    dma = pltpu.SemaphoreType.DMA

    def both(shape, kind=BF):
        return [pltpu.VMEM(shape(chunk), kind) for _, _, chunk in parts]

    pred, join, first, second, gin, emb = pl.pallas_call(
        functools.partial(step_kernel, parts, naz, nel, gates, rays, scale),
        out_shape=(
            jax.ShapeDtypeStruct((leads, n), F32),
            jax.ShapeDtypeStruct((C, C), F32),
            jax.ShapeDtypeStruct((9 * C, C), F32),
            jax.ShapeDtypeStruct((9 * C, C), F32),
            jax.ShapeDtypeStruct((inputs, C), F32),
            jax.ShapeDtypeStruct((sweeps, C), F32),
        ),
        in_specs=[pl.BlockSpec(memory_space=pltpu.SMEM)] + [vm] * 7,
        out_specs=(vm,) * 6,
        scratch_shapes=[
            pltpu.VMEM((64, n + 2 * h), BF),
            pltpu.VMEM((3 * C, n + 2 * h), BF),
            pltpu.VMEM((3 * C, (rays + 2 * D2) * gates), BF),
            pltpu.VMEM((3 * C, n + 2 * h), BF),
            pltpu.VMEM((3 * C, (rays + 2 * D1) * gates), BF),
        ]
        + both(lambda chunk: (naz * chunk, C), F32)
        + both(lambda chunk: (naz * chunk, C))
        + both(lambda chunk: (nq * chunk, C))
        + both(lambda chunk: (nq * chunk, C))
        + both(lambda chunk: (nq, chunk, C))
        + both(lambda chunk: (nel, chunk, C))
        + both(lambda chunk: (naz * chunk, C))
        + [
            pltpu.VMEM((nel, 16, n), F32),
            dma((2,)), dma((2,)),
            dma((2,)), dma((2,)),
            dma((2, nq)), dma((2, nq)),
            dma((2, nel)), dma((2, nel)),
            dma((2, nq)), dma((2, nq)),
            dma((2, nq)), dma((2, nq)),
            dma((nel,)), dma((nel,)),
        ],
        compiler_params=pltpu.CompilerParams(
            collective_id=0, has_side_effects=True, vmem_limit_bytes=48 * 1024 * 1024
        ),
        name="step",
    )(
        sweep_ids, xc, elevation_embed, proj,
        first_kernel.reshape(9 * C, C), second_kernel.reshape(9 * C, C),
        join_weight[0], head,
    )
    shape = first_kernel.shape
    return (
        pred.reshape(1, leads, rays, gates),
        join[None],
        first.reshape(shape),
        second.reshape(shape),
        gin,
        emb,
    )


def solution(mesh):
    in_specs = (
        P("el", None, None, "az", None),
        P("el"),
        P(),
        P(),
        P(),
        P(),
        P("el", None, None),
        P(),
        P(None, None, "az", None),
    )
    out_specs = (P(None, None, "az", None), P("el", None, None), P(), P(), P(), P())
    return jax.shard_map(shards, mesh=mesh, in_specs=in_specs, out_specs=out_specs, check_vma=False)
```

time: 67.2 us -> 48.6 us (0.72)
  the two profiles are of different devices: /device:TPU:27 before, /device:TPU:1 now
where the time goes in v2:
time: 48.6 us; the launch traced here: 48.4 us
  Pallas kernels  40.2 us (83%)
  local copies, waits for them, and re-layouts  6.59 us (14%)
  other arithmetic  0.87 us (2%)
  between operations  0.75 us (2%)
    pallas_call x1, Pallas kernels, shards(): pl.pallas_call(functools.partial(step_kernel, parts, naz, nel, gates, ray...  40.2 us
    unnamed x23, local copies, waits for them, and re-layouts  5.79 us

profile of v2, /device:TPU:1, one launch (start us, length us, event | category | flops | bytes accessed | tf_op | source)
XLA Modules:
  0.0 48.4 jit_solution(6720615689017299411)
XLA Ops:
  0.6 0.0 copy-start.6
  0.6 0.0 copy-start.5
  0.7 0.1 pad.9.clone
  0.7 0.6 %copy-done.6 = bf16[12,128]{1,0:T(8,128)(2,1)S(1)} copy-done((bf16[12,128]{1,0:T(8,128)(2,1)S(1)}, bf16[12,128]{1,0:T(8,128)(2,1)}, u32[]{:S(2)}) %copy-start.6) | copy-done | bytes 3096
  1.3 0.8 %pad_maximum_fusion.proj_ref = bf16[48,128]{1,0:T(8,128)(2,1)S(1)} fusion(bf16[24,128]{1,0:T(8,128)(2,1)} %param.12), kind=kLoop, calls=%fused_computation.1 | loop fusion | flops 24576 | bytes 18432 | tf_op jit(solution)/shard_map/concatenate | solution.py:339
  2.1 0.8 %pad.10 = bf16[16,6,256]{2,1,0:T(8,128)(2,1)S(1)} pad(bf16[12,6,256]{2,1,0:T(8,128)(2,1)} %bitcast.24, bf16[]{:T(256)} %constant.1.clone.1), padding=0_4x0_0x0_0 | pad | bytes 86018
  2.9 0.0 copy-done.5
  3.0 0.0 copy-start
  3.0 0.0 copy-start.1
  3.0 0.0 copy-start.2
  3.1 0.0 copy-start.3
  3.1 0.0 copy-start.4
  3.1 0.1 maximum_maximum_fusion.xc_ref
  3.2 0.8 %copy-done = bf16[3,3,128,128]{3,2,1,0:T(8,128)(2,1)S(1)} copy-done((bf16[3,3,128,128]{3,2,1,0:T(8,128)(2,1)S(1)}, bf16[3,3,128,128]{3,2,1,0:T(8,128)(2,1)}, u32[]{:S(2)}) %copy-start) | copy-done | bytes 294936
  3.9 0.1 copy-done.1
  4.0 0.0 copy-done.2
  4.0 0.0 copy-done.3
  4.0 40.2 %step.1 = (f32[12,1536]{1,0:T(8,128)S(1)}, f32[128,128]{1,0:T(8,128)S(1)}, f32[1152,128]{1,0:T(8,128)S(1)}, f32[1152,128]{1,0:T(8,128)S(1)}, f32[24,128]{1,0:T(8,128)S(1)}, /*index=5*/f32[4,128]{1,0:T(4,128)S(1)}) custom-call(s32[2]{0:T(128)S(1)} %copy-done.4, bf16[64,1536]{1,0:T(8,128)(2,1)S(1)} %maximum_maximum_fusion.xc_ref, f32[4,128]{1,0:T(4,128)S(1)} %copy-done.3, ...), custom_call_target="tpu_custom_call" | custom-call | tf_op jit(solution)/shard_map/step/pallas_call | solution.py:347
  44.2 0.7 %reshape.40 = f32[1,12,6,256]{3,0,2,1:T(1,128)} reshape(f32[12,1536]{1,0:T(8,128)S(1)} %get-tuple-element.12) | data formatting | bytes 147456 | tf_op jit(solution)/shard_map/reshape | solution.py:394
  45.0 0.6 %copy.26 = f32[1,128,128]{2,1,0:T(8,128)} copy(f32[1,128,128]{2,1,0:T(8,128)S(1)} %bitcast.18) | data formatting | bytes 131072
  45.6 0.8 %copy.27 = f32[3,3,128,128]{3,2,1,0:T(8,128)} copy(f32[3,3,128,128]{3,2,1,0:T(8,128)S(1)} %bitcast.15) | data formatting | bytes 1179648
  46.4 0.8 %copy.28 = f32[3,3,128,128]{3,2,1,0:T(8,128)} copy(f32[3,3,128,128]{3,2,1,0:T(8,128)S(1)} %bitcast.14) | data formatting | bytes 1179648
  47.2 0.6 %copy.29 = f32[24,128]{1,0:T(8,128)} copy(f32[24,128]{1,0:T(8,128)S(1)} %get-tuple-element.40) | data formatting | bytes 24576
  47.8 0.6 %copy.30 = f32[4,128]{1,0:T(4,128)} copy(f32[4,128]{1,0:T(4,128)S(1)} %get-tuple-element.41) | data formatting | bytes 4096
  (6 shorter events, 0.1 us)
Async XLA Ops:
  0.6 0.7 %copy-start.6 = (bf16[12,128]{1,0:T(8,128)(2,1)S(1)}, bf16[12,128]{1,0:T(8,128)(2,1)}, u32[]{:S(2)}) copy-start(bf16[12,128]{1,0:T(8,128)(2,1)} %param.16) | copy-start | bytes 9220
  0.6 2.3 %copy-start.5 = (bf16[2,1,24,6,256]{4,2,3,1,0:T(8,128)(2,1)S(1)}, bf16[2,1,24,6,256]{4,2,3,1,0:T(8,128)(2,1)}, u32[]{:S(2)}) copy-start(bf16[2,1,24,6,256]{4,2,3,1,0:T(8,128)(2,1)} %param.9) | copy-start | bytes 442372
  3.0 1.0 %copy-start = (bf16[3,3,128,128]{3,2,1,0:T(8,128)(2,1)S(1)}, bf16[3,3,128,128]{3,2,1,0:T(8,128)(2,1)}, u32[]{:S(2)}) copy-start(bf16[3,3,128,128]{3,2,1,0:T(8,128)(2,1)} %param.13) | copy-start | bytes 884740
  3.0 1.0 %copy-start.1 = (bf16[3,3,128,128]{3,2,1,0:T(8,128)(2,1)S(1)}, bf16[3,3,128,128]{3,2,1,0:T(8,128)(2,1)}, u32[]{:S(2)}) copy-start(bf16[3,3,128,128]{3,2,1,0:T(8,128)(2,1)} %param.14) | copy-start | bytes 884740
  3.0 1.0 %copy-start.2 = (bf16[1,128,128]{2,1,0:T(8,128)(2,1)S(1)}, bf16[1,128,128]{2,1,0:T(8,128)(2,1)}, u32[]{:S(2)}) copy-start(bf16[1,128,128]{2,1,0:T(8,128)(2,1)} %param.15) | copy-start | bytes 98308
  3.1 1.0 %copy-start.3 = (f32[4,128]{1,0:T(4,128)S(1)}, f32[4,128]{1,0:T(4,128)}, u32[]{:S(2)}) copy-start(f32[4,128]{1,0:T(4,128)} %embed_ref.1) | copy-start | bytes 6148
  3.1 1.0 %copy-start.4 = (s32[2]{0:T(128)S(1)}, s32[2]{0:T(128)}, u32[]{:S(2)}) copy-start(s32[2]{0:T(128)} %ids_ref.1) | copy-start | bytes 28

commit v3 on v2

--- a/solution.py
+++ b/solution.py
@@ -229,7 +229,9 @@
 
     up.wait_recv()
     down.wait_recv()
-    s0 = (dot(proj_ref[...], xe[0:48, :], TN) + bias).astype(BF).astype(F32)
+    proj = proj_ref[...].astype(F32)
+    proj = jnp.concatenate([proj] * slots, axis=0).astype(BF)
+    s0 = (dot(proj, xe[0:48, :], TN) + bias).astype(BF).astype(F32)
     fill_taps(t0, s0 * logistic(s0), D1, g)
 
     w1 = (rays + 2 * D2) * g
@@ -239,7 +241,7 @@
     s2 = s1[:, D2 * g : D2 * g + n] + conv(k2_ref, t1, 0, D2 * g, n)
     s2 = s2.astype(BF)
 
-    jb = dot(head_ref[...], xe[48:64, :], TN).astype(BF)
+    jb = dot(head_ref[...], xe[48:60, :], TN).astype(BF)
     join = dot(s2, jb[:, HALO * g : HALO * g + n], NT) * scale
     share, own, chunk = parts[0]
     for k in range(naz):
@@ -295,7 +297,7 @@
     pred = pbuf[0]
     for t in range(1, nel):
         pred = pred + pbuf[t]
-    pred_out[...] = pred[0 : pred_out.shape[0], :]
+    pred_out[...] = pred
     for c in e0:
         c.wait_recv()
     take(0, second_out, 0)
@@ -313,6 +315,22 @@
         c.wait_send()
 
 
+def write_kernel(*refs):
+    ins, outs, (lines, sems) = refs[0:6], refs[6:12], refs[12:14]
+    copies = [pltpu.make_async_copy(ins[i], outs[i], sems.at[i]) for i in range(1, 6)]
+    for c in copies:
+        c.start()
+    leads, n = ins[0].shape
+    tiles = n // C
+    for t in range(tiles):
+        lines[pl.ds(t, leads, stride=tiles), :] = ins[0][:, t * C : (t + 1) * C]
+    last = pltpu.make_async_copy(lines, outs[0], sems.at[0])
+    last.start()
+    for c in copies:
+        c.wait()
+    last.wait()
+
+
 def shards(
     raw_sweeps, sweep_ids, elevation_embed, input_proj, first_kernel, second_kernel,
     join_weight, head_weight, cotangent,
@@ -332,12 +350,9 @@
         [
             raw_sweeps.reshape(slots * inputs, n),
             cotangent.reshape(leads, n),
-            jnp.zeros((16 - leads, n), BF),
         ],
         axis=0,
     )
-    proj = jnp.concatenate([input_proj] * slots, axis=0)
-    head = jnp.pad(head_weight, ((0, 16 - leads), (0, 0)))
     vm = pl.BlockSpec(memory_space=pltpu.VMEM)
     dma = pltpu.SemaphoreType.DMA
 
@@ -357,7 +372,7 @@
         in_specs=[pl.BlockSpec(memory_space=pltpu.SMEM)] + [vm] * 7,
         out_specs=(vm,) * 6,
         scratch_shapes=[
-            pltpu.VMEM((64, n + 2 * h), BF),
+            pltpu.VMEM((60, n + 2 * h), BF),
             pltpu.VMEM((3 * C, n + 2 * h), BF),
             pltpu.VMEM((3 * C, (rays + 2 * D2) * gates), BF),
             pltpu.VMEM((3 * C, n + 2 * h), BF),
@@ -371,7 +386,7 @@
         + both(lambda chunk: (nel, chunk, C))
         + both(lambda chunk: (naz * chunk, C))
         + [
-            pltpu.VMEM((nel, 16, n), F32),
+            pltpu.VMEM((nel, leads, n), F32),
             dma((2,)), dma((2,)),
             dma((2,)), dma((2,)),
             dma((2, nq)), dma((2, nq)),
@@ -385,10 +400,22 @@
         ),
         name="step",
     )(
-        sweep_ids, xc, elevation_embed, proj,
+        sweep_ids, xc, elevation_embed, input_proj,
         first_kernel.reshape(9 * C, C), second_kernel.reshape(9 * C, C),
-        join_weight[0], head,
-    )
+        join_weight[0], head_weight,
+    )
+    tiles = n // C
+    arrays = (pred, join, first, second, gin, emb)
+    kinds = [jax.ShapeDtypeStruct((leads * tiles, C), F32)]
+    kinds += [jax.ShapeDtypeStruct(v.shape, F32) for v in arrays[1:]]
+    pred, join, first, second, gin, emb = pl.pallas_call(
+        write_kernel,
+        out_shape=tuple(kinds),
+        in_specs=[vm] * 6,
+        out_specs=(pl.BlockSpec(memory_space=pl.ANY),) * 6,
+        scratch_shapes=[pltpu.VMEM((leads * tiles, C), F32), dma((6,))],
+        name="write",
+    )(*arrays)
     shape = first_kernel.shape
     return (
         pred.reshape(1, leads, rays, gates),

time: 48.6 us -> 49.5 us (1.019)
  Pallas kernels: 40.2 us -> 42.6 us
  other arithmetic: 0.87 us -> 0.02 us
  local copies, waits for them, and re-layouts: 6.59 us -> 5.97 us
    pallas_call x0 -> x1, Pallas kernels: none -> 2.41 us  [shards(): pl.pallas_call(write_kernel, out_shape=tuple(kinds), in_specs=[vm] * 6, o...]
    concatenate x1 -> x0, other arithmetic: 0.77 us -> none  [shards(): proj = jnp.concatenate([input_proj] * slots, axis=0)]
    reshape x1 -> x0, local copies, waits for them, and re-layouts: 0.72 us -> none  [shards(): pred.reshape(1, leads, rays, gates)]
    unnamed x23 -> x32, local copies, waits for them, and re-layouts: 5.79 us -> 5.97 us
where the time goes in v3:
time: 49.5 us; the launch traced here: 49.3 us
  Pallas kernels  42.6 us (86%)
  local copies, waits for them, and re-layouts  5.97 us (12%)
  between operations  0.76 us (2%)
    pallas_call x1, Pallas kernels, shards(): pl.pallas_call(functools.partial(step_kernel, parts, naz, nel, gates, ray...  40.2 us
    unnamed x32, local copies, waits for them, and re-layouts  5.97 us
    pallas_call x1, Pallas kernels, shards(): pl.pallas_call(write_kernel, out_shape=tuple(kinds), in_specs=[vm] * 6, o...  2.41 us

profile of v3, /device:TPU:1, one launch (start us, length us, event | category | flops | bytes accessed | tf_op | source)
XLA Modules:
  0.0 49.3 jit_solution(10475947986780640711)
XLA Ops:
  0.6 0.0 copy-start.13
  0.6 0.8 %pad.2 = bf16[16,6,256]{2,1,0:T(8,128)(2,1)S(1)} pad(bf16[12,6,256]{2,1,0:T(8,128)(2,1)} %bitcast.22, bf16[]{:T(256)} %constant.4), padding=0_4x0_0x0_0 | pad | bytes 86018
  1.5 0.1 copy-done.13
  1.6 0.0 copy-start.2
  1.6 0.0 copy-start.3
  1.7 0.0 copy-start.6
  1.7 0.0 copy-start.8
  1.7 0.0 copy-start.9
  1.7 0.0 copy-start.10
  1.7 0.0 copy-start.12
  1.8 0.8 %copy-done.2 = bf16[3,3,128,128]{3,2,1,0:T(8,128)(2,1)S(1)} copy-done((bf16[3,3,128,128]{3,2,1,0:T(8,128)(2,1)S(1)}, bf16[3,3,128,128]{3,2,1,0:T(8,128)(2,1)}, u32[]{:S(2)}) %copy-start.2) | copy-done | bytes 294936
  2.6 0.1 copy-done.3
  2.7 0.0 copy-done.6
  2.7 0.0 copy-done.8
  2.7 0.0 copy-done.10
  2.7 40.2 %step.1 = (f32[12,1536]{1,0:T(8,128)S(1)}, f32[128,128]{1,0:T(8,128)S(1)}, f32[1152,128]{1,0:T(8,128)S(1)}, f32[1152,128]{1,0:T(8,128)S(1)}, f32[24,128]{1,0:T(8,128)S(1)}, /*index=5*/f32[4,128]{1,0:T(4,128)S(1)}) custom-call(s32[2]{0:T(128)S(1)} %copy-done.12, bf16[60,1536]{1,0:T(8,128)(2,1)S(1)} %pad_maximum_fusion.xc_ref, f32[4,128]{1,0:T(4,128)S(1)} %copy-done.10, ...), custom_call_target="tpu_custom_call" | custom-call | tf_op jit(solution)/shard_map/step/pallas_call | solution.py:362
  42.9 0.0 copy-start
  42.9 0.8 %copy-done = f32[1152,128]{1,0:T(8,128)} copy-done((f32[1152,128]{1,0:T(8,128)}, f32[1152,128]{1,0:T(8,128)S(1)}, u32[]{:S(2)}) %copy-start) | copy-done | bytes 589848
  43.7 0.8 %copy-done.1 = f32[1152,128]{1,0:T(8,128)} copy-done((f32[1152,128]{1,0:T(8,128)}, f32[1152,128]{1,0:T(8,128)S(1)}, u32[]{:S(2)}) %copy-start.1) | copy-done | bytes 589848
  44.5 0.6 %copy-done.4 = f32[12,1536]{1,0:T(8,128)} copy-done((f32[12,1536]{1,0:T(8,128)}, f32[12,1536]{1,0:T(8,128)S(1)}, u32[]{:S(2)}) %copy-start.4) | copy-done | bytes 73752
  45.1 0.6 %copy-done.5 = f32[128,128]{1,0:T(8,128)} copy-done((f32[128,128]{1,0:T(8,128)}, f32[128,128]{1,0:T(8,128)S(1)}, u32[]{:S(2)}) %copy-start.5) | copy-done | bytes 65560
  45.8 0.6 %copy-done.7 = f32[24,128]{1,0:T(8,128)} copy-done((f32[24,128]{1,0:T(8,128)}, f32[24,128]{1,0:T(8,128)S(1)}, u32[]{:S(2)}) %copy-start.7) | copy-done | bytes 12312
  46.4 0.6 %copy-done.11 = f32[4,128]{1,0:T(4,128)} copy-done((f32[4,128]{1,0:T(4,128)}, f32[4,128]{1,0:T(4,128)S(1)}, u32[]{:S(2)}) %copy-start.11) | copy-done | bytes 2072
  46.9 2.4 %write.1 = (f32[144,128]{1,0:T(8,128)}, f32[128,128]{1,0:T(8,128)}, f32[1152,128]{1,0:T(8,128)}, f32[1152,128]{1,0:T(8,128)}, f32[24,128]{1,0:T(8,128)}, /*index=5*/f32[4,128]{1,0:T(4,128)}) custom-call(f32[12,1536]{1,0:T(8,128)} %copy-done.4, f32[128,128]{1,0:T(8,128)} %copy-done.5, f32[1152,128]{1,0:T(8,128)} %copy-done, f32[1152,128]{1,0:T(8,128)} %copy-done.1, ...), custom_call_target="tpu_custom_call" | custom-call | tf_op jit(solution)/shard_map/write/pallas_call | solution.py:411
  (11 shorter events, 0.1 us)
Async XLA Ops:
  0.6 0.9 %copy-start.13 = (bf16[2,1,24,6,256]{4,2,3,1,0:T(8,128)(2,1)S(1)}, bf16[2,1,24,6,256]{4,2,3,1,0:T(8,128)(2,1)}, u32[]{:S(2)}) copy-start(bf16[2,1,24,6,256]{4,2,3,1,0:T(8,128)(2,1)} %param.9) | copy-start | bytes 442372
  1.6 1.0 %copy-start.2 = (bf16[3,3,128,128]{3,2,1,0:T(8,128)(2,1)S(1)}, bf16[3,3,128,128]{3,2,1,0:T(8,128)(2,1)}, u32[]{:S(2)}) copy-start(bf16[3,3,128,128]{3,2,1,0:T(8,128)(2,1)} %param.13) | copy-start | bytes 884740
  1.6 1.0 %copy-start.3 = (bf16[3,3,128,128]{3,2,1,0:T(8,128)(2,1)S(1)}, bf16[3,3,128,128]{3,2,1,0:T(8,128)(2,1)}, u32[]{:S(2)}) copy-start(bf16[3,3,128,128]{3,2,1,0:T(8,128)(2,1)} %param.14) | copy-start | bytes 884740
  1.7 1.0 %copy-start.6 = (bf16[1,128,128]{2,1,0:T(8,128)(2,1)S(1)}, bf16[1,128,128]{2,1,0:T(8,128)(2,1)}, u32[]{:S(2)}) copy-start(bf16[1,128,128]{2,1,0:T(8,128)(2,1)} %param.15) | copy-start | bytes 98308
  1.7 1.0 %copy-start.8 = (bf16[24,128]{1,0:T(8,128)(2,1)S(1)}, bf16[24,128]{1,0:T(8,128)(2,1)}, u32[]{:S(2)}) copy-start(bf16[24,128]{1,0:T(8,128)(2,1)} %proj_ref.1) | copy-start | bytes 18436
  1.7 1.0 %copy-start.9 = (bf16[12,128]{1,0:T(8,128)(2,1)S(1)}, bf16[12,128]{1,0:T(8,128)(2,1)}, u32[]{:S(2)}) copy-start(bf16[12,128]{1,0:T(8,128)(2,1)} %head_ref.1) | copy-start | bytes 9220
  1.7 1.0 %copy-start.10 = (f32[4,128]{1,0:T(4,128)S(1)}, f32[4,128]{1,0:T(4,128)}, u32[]{:S(2)}) copy-start(f32[4,128]{1,0:T(4,128)} %embed_ref.1) | copy-start | bytes 6148
  1.7 1.0 %copy-start.12 = (s32[2]{0:T(128)S(1)}, s32[2]{0:T(128)}, u32[]{:S(2)}) copy-start(s32[2]{0:T(128)} %ids_ref.1) | copy-start | bytes 28
  42.9 0.8 %copy-start = (f32[1152,128]{1,0:T(8,128)}, f32[1152,128]{1,0:T(8,128)S(1)}, u32[]{:S(2)}) copy-start(f32[1152,128]{1,0:T(8,128)S(1)} %get-tuple-element.20.refs_2_) | copy-start | bytes 1769476
  43.7 0.8 %copy-start.1 = (f32[1152,128]{1,0:T(8,128)}, f32[1152,128]{1,0:T(8,128)S(1)}, u32[]{:S(2)}) copy-start(f32[1152,128]{1,0:T(8,128)S(1)} %get-tuple-element.21.refs_3_) | copy-start | bytes 1769476
  44.5 0.6 %copy-start.4 = (f32[12,1536]{1,0:T(8,128)}, f32[12,1536]{1,0:T(8,128)S(1)}, u32[]{:S(2)}) copy-start(f32[12,1536]{1,0:T(8,128)S(1)} %get-tuple-element.18.refs_0_) | copy-start | bytes 221188
  45.1 0.6 %copy-start.5 = (f32[128,128]{1,0:T(8,128)}, f32[128,128]{1,0:T(8,128)S(1)}, u32[]{:S(2)}) copy-start(f32[128,128]{1,0:T(8,128)S(1)} %get-tuple-element.19.refs_1_) | copy-start | bytes 196612
  45.8 0.6 %copy-start.7 = (f32[24,128]{1,0:T(8,128)}, f32[24,128]{1,0:T(8,128)S(1)}, u32[]{:S(2)}) copy-start(f32[24,128]{1,0:T(8,128)S(1)} %get-tuple-element.22.refs_4_) | copy-start | bytes 36868
  46.4 0.6 %copy-start.11 = (f32[4,128]{1,0:T(4,128)}, f32[4,128]{1,0:T(4,128)S(1)}, u32[]{:S(2)}) copy-start(f32[4,128]{1,0:T(4,128)S(1)} %get-tuple-element.23.refs_5_) | copy-start | bytes 6148

commit v4 on v3

--- a/solution.py
+++ b/solution.py
@@ -414,6 +414,7 @@
         in_specs=[vm] * 6,
         out_specs=(pl.BlockSpec(memory_space=pl.ANY),) * 6,
         scratch_shapes=[pltpu.VMEM((leads * tiles, C), F32), dma((6,))],
+        compiler_params=pltpu.CompilerParams(vmem_limit_bytes=4 * 1024 * 1024),
         name="write",
     )(*arrays)
     shape = first_kernel.shape

time: 49.5 us -> 44.1 us (0.89)
  local copies, waits for them, and re-layouts: 5.97 us -> 1.93 us
  Pallas kernels: 42.6 us -> 41.3 us
    unnamed x32 -> x20, local copies, waits for them, and re-layouts: 5.97 us -> 1.93 us
    pallas_call x1, Pallas kernels: 2.41 us -> 1.11 us  [shards(): pl.pallas_call(write_kernel, out_shape=tuple(kinds), in_specs=[vm] * 6, o...]
where the time goes in v4:
time: 44.1 us; the launch traced here: 44 us
  Pallas kernels  41.3 us (94%)
  local copies, waits for them, and re-layouts  1.93 us (4%)
  between operations  0.75 us (2%)
    pallas_call x1, Pallas kernels, shards(): pl.pallas_call(functools.partial(step_kernel, parts, naz, nel, gates, ray...  40.2 us
    unnamed x20, local copies, waits for them, and re-layouts  1.93 us
    pallas_call x1, Pallas kernels, shards(): pl.pallas_call(write_kernel, out_shape=tuple(kinds), in_specs=[vm] * 6, o...  1.11 us

profile of v4, /device:TPU:1, one launch (start us, length us, event | category | flops | bytes accessed | tf_op | source)
XLA Modules:
  0.0 44.0 jit_solution(11021944437334303299)
XLA Ops:
  0.6 0.0 copy-start.7
  0.6 0.8 %pad.2 = bf16[16,6,256]{2,1,0:T(8,128)(2,1)S(1)} pad(bf16[12,6,256]{2,1,0:T(8,128)(2,1)} %bitcast.22, bf16[]{:T(256)} %constant.4), padding=0_4x0_0x0_0 | pad | bytes 86018
  1.5 0.1 copy-done.7
  1.6 0.0 copy-start
  1.6 0.0 copy-start.1
  1.7 0.0 copy-start.2
  1.7 0.0 copy-start.3
  1.7 0.0 copy-start.4
  1.7 0.0 copy-start.5
  1.7 0.0 copy-start.6
  1.8 0.8 %copy-done = bf16[3,3,128,128]{3,2,1,0:T(8,128)(2,1)S(1)} copy-done((bf16[3,3,128,128]{3,2,1,0:T(8,128)(2,1)S(1)}, bf16[3,3,128,128]{3,2,1,0:T(8,128)(2,1)}, u32[]{:S(2)}) %copy-start) | copy-done | bytes 294936
  2.6 0.1 copy-done.1
  2.7 0.0 copy-done.2
  2.7 0.0 copy-done.3
  2.7 0.0 copy-done.4
  2.7 0.0 copy-done.5
  2.7 0.0 copy-done.6
  2.7 40.2 %step.1 = (f32[12,1536]{1,0:T(8,128)S(1)}, f32[128,128]{1,0:T(8,128)S(1)}, f32[1152,128]{1,0:T(8,128)S(1)}, f32[1152,128]{1,0:T(8,128)S(1)}, f32[24,128]{1,0:T(8,128)S(1)}, /*index=5*/f32[4,128]{1,0:T(4,128)S(1)}) custom-call(s32[2]{0:T(128)S(1)} %copy-done.6, bf16[60,1536]{1,0:T(8,128)(2,1)S(1)} %pad_maximum_fusion.xc_ref, f32[4,128]{1,0:T(4,128)S(1)} %copy-done.5, ...), custom_call_target="tpu_custom_call" | custom-call | tf_op jit(solution)/shard_map/step/pallas_call | solution.py:362
  42.9 1.1 %write.1 = (f32[144,128]{1,0:T(8,128)}, f32[128,128]{1,0:T(8,128)}, f32[1152,128]{1,0:T(8,128)}, f32[1152,128]{1,0:T(8,128)}, f32[24,128]{1,0:T(8,128)}, /*index=5*/f32[4,128]{1,0:T(4,128)}) custom-call(f32[12,1536]{1,0:T(8,128)S(1)} %get-tuple-element.18.refs_0_, f32[128,128]{1,0:T(8,128)S(1)} %get-tuple-element.19.refs_1_, ...), custom_call_target="tpu_custom_call" | custom-call | tf_op jit(solution)/shard_map/write/pallas_call | solution.py:411
  (4 shorter events, 0.1 us)
Async XLA Ops:
  0.6 0.9 %copy-start.7 = (bf16[2,1,24,6,256]{4,2,3,1,0:T(8,128)(2,1)S(1)}, bf16[2,1,24,6,256]{4,2,3,1,0:T(8,128)(2,1)}, u32[]{:S(2)}) copy-start(bf16[2,1,24,6,256]{4,2,3,1,0:T(8,128)(2,1)} %param.9) | copy-start | bytes 442372
  1.6 1.0 %copy-start = (bf16[3,3,128,128]{3,2,1,0:T(8,128)(2,1)S(1)}, bf16[3,3,128,128]{3,2,1,0:T(8,128)(2,1)}, u32[]{:S(2)}) copy-start(bf16[3,3,128,128]{3,2,1,0:T(8,128)(2,1)} %param.13) | copy-start | bytes 884740
  1.6 1.0 %copy-start.1 = (bf16[3,3,128,128]{3,2,1,0:T(8,128)(2,1)S(1)}, bf16[3,3,128,128]{3,2,1,0:T(8,128)(2,1)}, u32[]{:S(2)}) copy-start(bf16[3,3,128,128]{3,2,1,0:T(8,128)(2,1)} %param.14) | copy-start | bytes 884740
  1.7 1.0 %copy-start.2 = (bf16[1,128,128]{2,1,0:T(8,128)(2,1)S(1)}, bf16[1,128,128]{2,1,0:T(8,128)(2,1)}, u32[]{:S(2)}) copy-start(bf16[1,128,128]{2,1,0:T(8,128)(2,1)} %param.15) | copy-start | bytes 98308
  1.7 1.0 %copy-start.3 = (bf16[24,128]{1,0:T(8,128)(2,1)S(1)}, bf16[24,128]{1,0:T(8,128)(2,1)}, u32[]{:S(2)}) copy-start(bf16[24,128]{1,0:T(8,128)(2,1)} %proj_ref.1) | copy-start | bytes 18436
  1.7 1.0 %copy-start.4 = (bf16[12,128]{1,0:T(8,128)(2,1)S(1)}, bf16[12,128]{1,0:T(8,128)(2,1)}, u32[]{:S(2)}) copy-start(bf16[12,128]{1,0:T(8,128)(2,1)} %head_ref.1) | copy-start | bytes 9220
  1.7 1.0 %copy-start.5 = (f32[4,128]{1,0:T(4,128)S(1)}, f32[4,128]{1,0:T(4,128)}, u32[]{:S(2)}) copy-start(f32[4,128]{1,0:T(4,128)} %embed_ref.1) | copy-start | bytes 6148
  1.7 1.0 %copy-start.6 = (s32[2]{0:T(128)S(1)}, s32[2]{0:T(128)}, u32[]{:S(2)}) copy-start(s32[2]{0:T(128)} %ids_ref.1) | copy-start | bytes 28

commit v5 on v4

--- a/solution.py
+++ b/solution.py
@@ -41,11 +41,11 @@
     return s * (1.0 + v * (1.0 - s))
 
 
-def layouts(sweeps, naz):
+def layouts(sweeps, naz, nel):
+    count = naz * nel
     own = C // naz
-    share = up8(-(-9 * C // naz))
-    chunk = up16(share + own)
-    rest = up16(-(-(9 * C + 24 + up8(sweeps)) // naz))
+    chunk = up16(up8(-(-9 * C // count)) + own)
+    rest = up16(-(-(9 * C + 24 + up8(sweeps)) // count))
     return (chunk - own, own, chunk), (rest, 0, rest)
 
 
@@ -76,11 +76,12 @@
     pred_out, join_out, first_out, second_out, input_out, embed_out,
     xe, t0, t1, tu2, tu1,
     pack0, pack1, pay0, pay1, abuf0, abuf1, half0, half1,
-    rbuf0, rbuf1, mbuf0, mbuf1, gbuf0, gbuf1, pbuf,
-    sh, rh, sa, ra, sb, rb, sc, rc, sd, rd, se, re, sp, rp,
+    block0, block1, ybuf0, ybuf1, rbuf0, rbuf1, gbuf0, gbuf1, pbuf,
+    sh, rh, sa, ra, sb, rb, sc, rc, sd, rd, sy, ry, se, re, sp, rp,
 ):
     packs, pays, abufs, halves = (pack0, pack1), (pay0, pay1), (abuf0, abuf1), (half0, half1)
-    rbufs, mbufs, gbufs = (rbuf0, rbuf1), (mbuf0, mbuf1), (gbuf0, gbuf1)
+    rbufs, ybufs, gbufs = (rbuf0, rbuf1), (ybuf0, ybuf1), (gbuf0, gbuf1)
+    blocks = (block0, block1)
     g = gates
     n = rays * g
     h = HALO * g
@@ -129,63 +130,78 @@
         for src, dst, size in pieces(start, value.shape[0], share, chunk):
             packs[i][dst : dst + size, :] = value[src : src + size, :]
 
+    def place(c_, e_, q_):
+        return (c_ * nel + e_) * nq + q_
+
     def phase_a(i):
-        chunk = parts[i][2]
+        size = nel * nq * parts[i][2]
         pays[i][...] = packs[i][...].astype(BF)
         return send(
-            pays[i].at[rows(1 - core, nq * chunk), :], abufs[i], sa.at[i], ra.at[i], partner
+            pays[i].at[rows(1 - core, size), :], abufs[i], sa.at[i], ra.at[i], partner
         )
 
-    def phase_b(i, arrived):
+    def phase_y(i, arrived):
         chunk = parts[i][2]
         arrived.wait_recv()
-        mine = pays[i][rows(core, nq * chunk), :].astype(F32)
+        mine = pays[i][rows(core, nel * nq * chunk), :].astype(F32)
         halves[i][...] = (mine + abufs[i][...].astype(F32)).astype(BF)
         return [
             send(
-                halves[i].at[rows(lax.rem(q + s, nq), chunk), :], rbufs[i].at[s],
+                halves[i].at[rows(lax.rem(e + t, nel), nq * chunk), :], ybufs[i].at[t],
+                sc.at[i, t], rc.at[i, t], column[t],
+            )
+            for t in range(1, nel)
+        ]
+
+    def phase_b(i, arrived):
+        chunk = parts[i][2]
+        total = halves[i][rows(e, nq * chunk), :].astype(F32)
+        for t in range(1, nel):
+            arrived[t - 1].wait_recv()
+            total = total + ybufs[i][t].astype(F32)
+        blocks[i][...] = total.astype(BF)
+        return [
+            send(
+                blocks[i].at[rows(lax.rem(q + s, nq), chunk), :], rbufs[i].at[s],
                 sb.at[i, s], rb.at[i, s], same[s],
             )
             for s in range(1, nq)
         ]
 
-    def phase_c(i, arrived):
+    def share_line(i, s, view):
+        return [
+            send(view, view, sy.at[i, s, t], ry.at[i, s, t], column[t]) for t in range(1, nel)
+        ]
+
+    def phase_d(i, arrived):
         chunk = parts[i][2]
-        acc = halves[i][rows(q, chunk), :].astype(F32)
+        total = blocks[i][rows(q, chunk), :].astype(F32)
         for s in range(1, nq):
             arrived[s - 1].wait_recv()
-            acc = acc + rbufs[i][s].astype(F32)
-        mbufs[i][e] = acc.astype(BF)
-        sent = [
-            send(mbufs[i].at[e], mbufs[i].at[e], sc.at[i, t], rc.at[i, t], column[t])
-            for t in range(1, nel)
-        ]
-        return acc, sent
-
-    def phase_d(i, acc, arrived):
-        share, own, chunk = parts[i]
-        for c in arrived:
-            c.wait_recv()
-        total = mbufs[i][0].astype(F32)
-        for t in range(1, nel):
-            total = total + mbufs[i][t].astype(F32)
-        if own:
-            line = lax.broadcasted_iota(jnp.int32, total.shape, 0)
-            total = jnp.where(line < share, total, acc)
-        mine = rows(core * nq + q, chunk)
+            total = total + rbufs[i][s].astype(F32)
+        mine = rows(place(core, e, q), chunk)
         gbufs[i][mine, :] = total.astype(BF)
         view = gbufs[i].at[mine, :]
         sent = [send(view, view, sd.at[i, s], rd.at[i, s], same[s]) for s in range(1, nq)]
-        own_sent = send(view, view, se.at[i, 0], re.at[i, 0], partner)
-        return sent, own_sent
-
-    def phase_e(i, arrived, own_sent):
+        return sent, share_line(i, 0, view)
+
+    def phase_e(i, arrived, lines):
         chunk = parts[i][2]
-        last = [own_sent]
         for s in range(1, nq):
             arrived[s - 1].wait_recv()
-            view = gbufs[i].at[rows(core * nq + lax.rem(q + nq - s, nq), chunk), :]
-            last.append(send(view, view, se.at[i, s], re.at[i, s], partner))
+            m = place(core, e, lax.rem(q + nq - s, nq))
+            lines = lines + share_line(i, s, gbufs[i].at[rows(m, chunk), :])
+        view = gbufs[i].at[rows(core * nel + e, nq * chunk), :]
+        return lines, send(view, view, se.at[i, 0], re.at[i, 0], partner)
+
+    def phase_f(i, lines, last):
+        size = nq * parts[i][2]
+        last = [last]
+        for c in lines:
+            c.wait_recv()
+        for t in range(1, nel):
+            view = gbufs[i].at[rows(core * nel + lax.rem(e + nel - t, nel), size), :]
+            last.append(send(view, view, se.at[i, t], re.at[i, t], partner))
         return last
 
     def take(i, ref, start):
@@ -245,7 +261,8 @@
     join = dot(s2, jb[:, HALO * g : HALO * g + n], NT) * scale
     share, own, chunk = parts[0]
     for k in range(naz):
-        packs[0][k * chunk + share : (k + 1) * chunk, :] = join[k * own : (k + 1) * own, :]
+        first = pl.multiple_of(place(k // nq, e, k % nq) * chunk + share, 8)
+        packs[0][pl.ds(first, own), :] = join[k * own : (k + 1) * own, :]
 
     g2 = dot(wj_ref[...], jb, NN)
     fill_taps(tu2, g2, D2, g)
@@ -263,12 +280,13 @@
     g1 = g2[:, D2 * g : D2 * g + wb] + back(k2_ref, tu2, D2 * g, wb) * slope(
         s1[:, (D2 - D1) * g : (D2 - D1) * g + wb]
     )
-    b0 = phase_b(0, a0)
+    y0 = phase_y(0, a0)
     fill_taps(tu1, g1, D1, g)
     for p in range(3):
         first = (HALO + D1 * (p - 1)) * g
         part = dot(t0[:, first : first + n], tu1[C : 2 * C, D1 * g : D1 * g + n], NT)
         put(1, p * 3 * C, part * scale)
+    b0 = phase_b(0, y0)
     g0 = g1[:, D1 * g : D1 * g + n] + back(k1_ref, tu1, D1 * g, n) * slope(
         s0[:, HALO * g : HALO * g + n]
     )
@@ -283,30 +301,30 @@
         grads = grads + jnp.where(index == s, owns[s] * summed, 0.0)
     put(1, 9 * C + 24, grads)
     a1 = phase_a(1)
-    acc0, c0 = phase_c(0, b0)
-    b1 = phase_b(1, a1)
-    d0, own0 = phase_d(0, acc0, c0)
+    d0, l0 = phase_d(0, b0)
+    y1 = phase_y(1, a1)
     preds = [
         send(pbuf.at[e], pbuf.at[e], sp.at[t], rp.at[t], column[t]) for t in range(1, nel)
     ]
-    acc1, c1 = phase_c(1, b1)
-    d1, own1 = phase_d(1, acc1, c1)
-    e0 = phase_e(0, d0, own0)
+    b1 = phase_b(1, y1)
+    l0, e0 = phase_e(0, d0, l0)
+    d1, l1 = phase_d(1, b1)
+    f0 = phase_f(0, l0, e0)
     for c in preds:
         c.wait_recv()
     pred = pbuf[0]
     for t in range(1, nel):
         pred = pred + pbuf[t]
     pred_out[...] = pred
-    for c in e0:
+    for c in f0:
         c.wait_recv()
     take(0, second_out, 0)
     for k in range(naz):
-        join_out[k * own : (k + 1) * own, :] = gbufs[0][
-            k * chunk + share : (k + 1) * chunk, :
-        ].astype(F32)
-    e1 = phase_e(1, d1, own1)
-    for c in e1:
+        line = gbufs[0][rows(place(k // nq, e, k % nq), chunk), :].astype(F32)
+        join_out[k * own : (k + 1) * own, :] = line[share : share + own, :]
+    l1, e1 = phase_e(1, d1, l1)
+    f1 = phase_f(1, l1, e1)
+    for c in f1:
         c.wait_recv()
     take(1, first_out, 0)
     take(1, input_out, 9 * C)
@@ -340,7 +358,7 @@
     slots, _, inputs, rays, gates = raw_sweeps.shape
     leads = head_weight.shape[0]
     sweeps = elevation_embed.shape[0]
-    parts = layouts(sweeps, naz)
+    parts = layouts(sweeps, naz, nel)
     scale = 1.0 / math.sqrt(nel * rays * naz * gates)
     n = rays * gates
     h = HALO * gates
@@ -378,13 +396,14 @@
             pltpu.VMEM((3 * C, n + 2 * h), BF),
             pltpu.VMEM((3 * C, (rays + 2 * D1) * gates), BF),
         ]
-        + both(lambda chunk: (naz * chunk, C), F32)
-        + both(lambda chunk: (naz * chunk, C))
+        + both(lambda chunk: (naz * nel * chunk, C), F32)
+        + both(lambda chunk: (naz * nel * chunk, C))
+        + both(lambda chunk: (nq * nel * chunk, C))
+        + both(lambda chunk: (nq * nel * chunk, C))
         + both(lambda chunk: (nq * chunk, C))
-        + both(lambda chunk: (nq * chunk, C))
+        + both(lambda chunk: (nel, nq * chunk, C))
         + both(lambda chunk: (nq, chunk, C))
-        + both(lambda chunk: (nel, chunk, C))
-        + both(lambda chunk: (naz * chunk, C))
+        + both(lambda chunk: (naz * nel * chunk, C))
         + [
             pltpu.VMEM((nel, leads, n), F32),
             dma((2,)), dma((2,)),
@@ -392,7 +411,8 @@
             dma((2, nq)), dma((2, nq)),
             dma((2, nel)), dma((2, nel)),
             dma((2, nq)), dma((2, nq)),
-            dma((2, nq)), dma((2, nq)),
+            dma((2, nq, nel)), dma((2, nq, nel)),
+            dma((2, nel)), dma((2, nel)),
             dma((nel,)), dma((nel,)),
         ],
         compiler_params=pltpu.CompilerParams(

time: 44.1 us -> 51.4 us (1.17)
  Pallas kernels: 41.3 us -> 48.5 us
    pallas_call x1, Pallas kernels: 40.2 us -> 47.4 us  [shards(): pl.pallas_call(functools.partial(step_kernel, parts, naz, nel, gates, ray...]
where the time goes in v5:
time: 51.4 us; the launch traced here: 51.2 us
  Pallas kernels  48.5 us (94%)
  local copies, waits for them, and re-layouts  1.93 us (4%)
  between operations  0.75 us (1%)
    pallas_call x1, Pallas kernels, shards(): pl.pallas_call(functools.partial(step_kernel, parts, naz, nel, gates, ray...  47.4 us
    unnamed x20, local copies, waits for them, and re-layouts  1.93 us
    pallas_call x1, Pallas kernels, shards(): pl.pallas_call(write_kernel, out_shape=tuple(kinds), in_specs=[vm] * 6, o...  1.11 us

profile of v5, /device:TPU:1, one launch (start us, length us, event | category | flops | bytes accessed | tf_op | source)
XLA Modules:
  0.0 51.2 jit_solution(2663858828067738088)
XLA Ops:
  0.6 0.0 copy-start.7
  0.6 0.8 %pad.2 = bf16[16,6,256]{2,1,0:T(8,128)(2,1)S(1)} pad(bf16[12,6,256]{2,1,0:T(8,128)(2,1)} %bitcast.22, bf16[]{:T(256)} %constant.4), padding=0_4x0_0x0_0 | pad | bytes 86018
  1.5 0.1 copy-done.7
  1.6 0.0 copy-start
  1.6 0.0 copy-start.1
  1.7 0.0 copy-start.2
  1.7 0.0 copy-start.3
  1.7 0.0 copy-start.4
  1.7 0.0 copy-start.5
  1.7 0.0 copy-start.6
  1.8 0.8 %copy-done = bf16[3,3,128,128]{3,2,1,0:T(8,128)(2,1)S(1)} copy-done((bf16[3,3,128,128]{3,2,1,0:T(8,128)(2,1)S(1)}, bf16[3,3,128,128]{3,2,1,0:T(8,128)(2,1)}, u32[]{:S(2)}) %copy-start) | copy-done | bytes 294936
  2.6 0.1 copy-done.1
  2.7 0.0 copy-done.2
  2.7 0.0 copy-done.3
  2.7 0.0 copy-done.4
  2.7 0.0 copy-done.5
  2.7 0.0 copy-done.6
  2.7 47.4 %step.1 = (f32[12,1536]{1,0:T(8,128)S(1)}, f32[128,128]{1,0:T(8,128)S(1)}, f32[1152,128]{1,0:T(8,128)S(1)}, f32[1152,128]{1,0:T(8,128)S(1)}, f32[24,128]{1,0:T(8,128)S(1)}, /*index=5*/f32[4,128]{1,0:T(4,128)S(1)}) custom-call(s32[2]{0:T(128)S(1)} %copy-done.6, bf16[60,1536]{1,0:T(8,128)(2,1)S(1)} %pad_maximum_fusion.xc_ref, f32[4,128]{1,0:T(4,128)S(1)} %copy-done.5, ...), custom_call_target="tpu_custom_call" | custom-call | tf_op jit(solution)/shard_map/step/pallas_call | solution.py:380
  50.1 1.1 %write.1 = (f32[144,128]{1,0:T(8,128)}, f32[128,128]{1,0:T(8,128)}, f32[1152,128]{1,0:T(8,128)}, f32[1152,128]{1,0:T(8,128)}, f32[24,128]{1,0:T(8,128)}, /*index=5*/f32[4,128]{1,0:T(4,128)}) custom-call(f32[12,1536]{1,0:T(8,128)S(1)} %get-tuple-element.18.refs_0_, f32[128,128]{1,0:T(8,128)S(1)} %get-tuple-element.19.refs_1_, ...), custom_call_target="tpu_custom_call" | custom-call | tf_op jit(solution)/shard_map/write/pallas_call | solution.py:431
  (4 shorter events, 0.1 us)
Async XLA Ops:
  0.6 0.9 %copy-start.7 = (bf16[2,1,24,6,256]{4,2,3,1,0:T(8,128)(2,1)S(1)}, bf16[2,1,24,6,256]{4,2,3,1,0:T(8,128)(2,1)}, u32[]{:S(2)}) copy-start(bf16[2,1,24,6,256]{4,2,3,1,0:T(8,128)(2,1)} %param.9) | copy-start | bytes 442372
  1.6 1.0 %copy-start = (bf16[3,3,128,128]{3,2,1,0:T(8,128)(2,1)S(1)}, bf16[3,3,128,128]{3,2,1,0:T(8,128)(2,1)}, u32[]{:S(2)}) copy-start(bf16[3,3,128,128]{3,2,1,0:T(8,128)(2,1)} %param.13) | copy-start | bytes 884740
  1.6 1.0 %copy-start.1 = (bf16[3,3,128,128]{3,2,1,0:T(8,128)(2,1)S(1)}, bf16[3,3,128,128]{3,2,1,0:T(8,128)(2,1)}, u32[]{:S(2)}) copy-start(bf16[3,3,128,128]{3,2,1,0:T(8,128)(2,1)} %param.14) | copy-start | bytes 884740
  1.7 1.0 %copy-start.2 = (bf16[1,128,128]{2,1,0:T(8,128)(2,1)S(1)}, bf16[1,128,128]{2,1,0:T(8,128)(2,1)}, u32[]{:S(2)}) copy-start(bf16[1,128,128]{2,1,0:T(8,128)(2,1)} %param.15) | copy-start | bytes 98308
  1.7 1.0 %copy-start.3 = (bf16[24,128]{1,0:T(8,128)(2,1)S(1)}, bf16[24,128]{1,0:T(8,128)(2,1)}, u32[]{:S(2)}) copy-start(bf16[24,128]{1,0:T(8,128)(2,1)} %proj_ref.1) | copy-start | bytes 18436
  1.7 1.0 %copy-start.4 = (bf16[12,128]{1,0:T(8,128)(2,1)S(1)}, bf16[12,128]{1,0:T(8,128)(2,1)}, u32[]{:S(2)}) copy-start(bf16[12,128]{1,0:T(8,128)(2,1)} %head_ref.1) | copy-start | bytes 9220
  1.7 1.0 %copy-start.5 = (f32[4,128]{1,0:T(4,128)S(1)}, f32[4,128]{1,0:T(4,128)}, u32[]{:S(2)}) copy-start(f32[4,128]{1,0:T(4,128)} %embed_ref.1) | copy-start | bytes 6148
  1.7 1.0 %copy-start.6 = (s32[2]{0:T(128)S(1)}, s32[2]{0:T(128)}, u32[]{:S(2)}) copy-start(s32[2]{0:T(128)} %ids_ref.1) | copy-start | bytes 28

commit v6 on v4

--- a/solution.py
+++ b/solution.py
@@ -176,17 +176,13 @@
         gbufs[i][mine, :] = total.astype(BF)
         view = gbufs[i].at[mine, :]
         sent = [send(view, view, sd.at[i, s], rd.at[i, s], same[s]) for s in range(1, nq)]
-        own_sent = send(view, view, se.at[i, 0], re.at[i, 0], partner)
-        return sent, own_sent
-
-    def phase_e(i, arrived, own_sent):
-        chunk = parts[i][2]
-        last = [own_sent]
-        for s in range(1, nq):
-            arrived[s - 1].wait_recv()
-            view = gbufs[i].at[rows(core * nq + lax.rem(q + nq - s, nq), chunk), :]
-            last.append(send(view, view, se.at[i, s], re.at[i, s], partner))
-        return last
+        return sent
+
+    def phase_e(i, arrived):
+        for c in arrived:
+            c.wait_recv()
+        view = gbufs[i].at[rows(core, nq * parts[i][2]), :]
+        return [send(view, view, se.at[i, 0], re.at[i, 0], partner)]
 
     def take(i, ref, start):
         share, own, chunk = parts[i]
@@ -285,13 +281,13 @@
     a1 = phase_a(1)
     acc0, c0 = phase_c(0, b0)
     b1 = phase_b(1, a1)
-    d0, own0 = phase_d(0, acc0, c0)
+    d0 = phase_d(0, acc0, c0)
     preds = [
         send(pbuf.at[e], pbuf.at[e], sp.at[t], rp.at[t], column[t]) for t in range(1, nel)
     ]
     acc1, c1 = phase_c(1, b1)
-    d1, own1 = phase_d(1, acc1, c1)
-    e0 = phase_e(0, d0, own0)
+    d1 = phase_d(1, acc1, c1)
+    e0 = phase_e(0, d0)
     for c in preds:
         c.wait_recv()
     pred = pbuf[0]
@@ -305,7 +301,7 @@
         join_out[k * own : (k + 1) * own, :] = gbufs[0][
             k * chunk + share : (k + 1) * chunk, :
         ].astype(F32)
-    e1 = phase_e(1, d1, own1)
+    e1 = phase_e(1, d1)
     for c in e1:
         c.wait_recv()
     take(1, first_out, 0)

time: 44.1 us -> 44.1 us (level)
  no operation moved by 1% of the time
where the time goes in v6:
time: 44.1 us; the launch traced here: 44 us
  Pallas kernels  41.3 us (94%)
  local copies, waits for them, and re-layouts  1.93 us (4%)
  between operations  0.75 us (2%)
    pallas_call x1, Pallas kernels, shards(): pl.pallas_call(functools.partial(step_kernel, parts, naz, nel, gates, ray...  40.2 us
    unnamed x20, local copies, waits for them, and re-layouts  1.93 us
    pallas_call x1, Pallas kernels, shards(): pl.pallas_call(write_kernel, out_shape=tuple(kinds), in_specs=[vm] * 6, o...  1.11 us

profile of v6, /device:TPU:1, one launch (start us, length us, event | category | flops | bytes accessed | tf_op | source)
XLA Modules:
  0.0 44.0 jit_solution(6940186381528821643)
XLA Ops:
  0.6 0.0 copy-start.7
  0.6 0.8 %pad.2 = bf16[16,6,256]{2,1,0:T(8,128)(2,1)S(1)} pad(bf16[12,6,256]{2,1,0:T(8,128)(2,1)} %bitcast.22, bf16[]{:T(256)} %constant.4), padding=0_4x0_0x0_0 | pad | bytes 86018
  1.5 0.1 copy-done.7
  1.6 0.0 copy-start
  1.6 0.0 copy-start.1
  1.7 0.0 copy-start.2
  1.7 0.0 copy-start.3
  1.7 0.0 copy-start.4
  1.7 0.0 copy-start.5
  1.7 0.0 copy-start.6
  1.8 0.8 %copy-done = bf16[3,3,128,128]{3,2,1,0:T(8,128)(2,1)S(1)} copy-done((bf16[3,3,128,128]{3,2,1,0:T(8,128)(2,1)S(1)}, bf16[3,3,128,128]{3,2,1,0:T(8,128)(2,1)}, u32[]{:S(2)}) %copy-start) | copy-done | bytes 294936
  2.6 0.1 copy-done.1
  2.7 0.0 copy-done.2
  2.7 0.0 copy-done.3
  2.7 0.0 copy-done.4
  2.7 0.0 copy-done.5
  2.7 0.0 copy-done.6
  2.7 40.2 %step.1 = (f32[12,1536]{1,0:T(8,128)S(1)}, f32[128,128]{1,0:T(8,128)S(1)}, f32[1152,128]{1,0:T(8,128)S(1)}, f32[1152,128]{1,0:T(8,128)S(1)}, f32[24,128]{1,0:T(8,128)S(1)}, /*index=5*/f32[4,128]{1,0:T(4,128)S(1)}) custom-call(s32[2]{0:T(128)S(1)} %copy-done.6, bf16[60,1536]{1,0:T(8,128)(2,1)S(1)} %pad_maximum_fusion.xc_ref, f32[4,128]{1,0:T(4,128)S(1)} %copy-done.5, ...), custom_call_target="tpu_custom_call" | custom-call | tf_op jit(solution)/shard_map/step/pallas_call | solution.py:358
  42.9 1.1 %write.1 = (f32[144,128]{1,0:T(8,128)}, f32[128,128]{1,0:T(8,128)}, f32[1152,128]{1,0:T(8,128)}, f32[1152,128]{1,0:T(8,128)}, f32[24,128]{1,0:T(8,128)}, /*index=5*/f32[4,128]{1,0:T(4,128)}) custom-call(f32[12,1536]{1,0:T(8,128)S(1)} %get-tuple-element.18.refs_0_, f32[128,128]{1,0:T(8,128)S(1)} %get-tuple-element.19.refs_1_, ...), custom_call_target="tpu_custom_call" | custom-call | tf_op jit(solution)/shard_map/write/pallas_call | solution.py:407
  (4 shorter events, 0.1 us)
Async XLA Ops:
  0.6 0.9 %copy-start.7 = (bf16[2,1,24,6,256]{4,2,3,1,0:T(8,128)(2,1)S(1)}, bf16[2,1,24,6,256]{4,2,3,1,0:T(8,128)(2,1)}, u32[]{:S(2)}) copy-start(bf16[2,1,24,6,256]{4,2,3,1,0:T(8,128)(2,1)} %param.9) | copy-start | bytes 442372
  1.6 1.0 %copy-start = (bf16[3,3,128,128]{3,2,1,0:T(8,128)(2,1)S(1)}, bf16[3,3,128,128]{3,2,1,0:T(8,128)(2,1)}, u32[]{:S(2)}) copy-start(bf16[3,3,128,128]{3,2,1,0:T(8,128)(2,1)} %param.13) | copy-start | bytes 884740
  1.6 1.0 %copy-start.1 = (bf16[3,3,128,128]{3,2,1,0:T(8,128)(2,1)S(1)}, bf16[3,3,128,128]{3,2,1,0:T(8,128)(2,1)}, u32[]{:S(2)}) copy-start(bf16[3,3,128,128]{3,2,1,0:T(8,128)(2,1)} %param.14) | copy-start | bytes 884740
  1.7 1.0 %copy-start.2 = (bf16[1,128,128]{2,1,0:T(8,128)(2,1)S(1)}, bf16[1,128,128]{2,1,0:T(8,128)(2,1)}, u32[]{:S(2)}) copy-start(bf16[1,128,128]{2,1,0:T(8,128)(2,1)} %param.15) | copy-start | bytes 98308
  1.7 1.0 %copy-start.3 = (bf16[24,128]{1,0:T(8,128)(2,1)S(1)}, bf16[24,128]{1,0:T(8,128)(2,1)}, u32[]{:S(2)}) copy-start(bf16[24,128]{1,0:T(8,128)(2,1)} %proj_ref.1) | copy-start | bytes 18436
  1.7 1.0 %copy-start.4 = (bf16[12,128]{1,0:T(8,128)(2,1)S(1)}, bf16[12,128]{1,0:T(8,128)(2,1)}, u32[]{:S(2)}) copy-start(bf16[12,128]{1,0:T(8,128)(2,1)} %head_ref.1) | copy-start | bytes 9220
  1.7 1.0 %copy-start.5 = (f32[4,128]{1,0:T(4,128)S(1)}, f32[4,128]{1,0:T(4,128)}, u32[]{:S(2)}) copy-start(f32[4,128]{1,0:T(4,128)} %embed_ref.1) | copy-start | bytes 6148
  1.7 1.0 %copy-start.6 = (s32[2]{0:T(128)S(1)}, s32[2]{0:T(128)}, u32[]{:S(2)}) copy-start(s32[2]{0:T(128)} %ids_ref.1) | copy-start | bytes 28
